TPU v7x, 128 devices: a whole 4x4x4 slice. The times are simulated.
128 devices in a mesh: band: 8 (over z_hi, x), slab: 16 (over z_lo, y, core).
Axes of the slice: x: 4, y: 4, z: 4 (z_hi: 2, z_lo: 2; z = z_hi * 2 + z_lo), core: 2. Of those that a mesh axis runs over, the one named last changes fastest.
Arguments:
- orbitals: bfloat16 [32, 256, 256, 256], P('band', 'slab'), may hold values from -6 to 6
- occupation: float32 [32], P('band'), may hold values from 0.2 to 2
Outputs:
- density: float32 [256, 256, 256], P('slab', 'band')
- hartree: float32 [256, 256, 256], P('slab', 'band')
All inputs are finite; a program needn't handle non-finite values.
Results may differ from a plain program's by a relative error of at most 0.0019.
Values sent between devices are 32-bit elements; how exact they have to be, the bound alone decides.
No kernel may reach another device: no remote copies, remote signals or barrier semaphores. Data moves between devices by JAX's collectives and lax.ppermute only.
A program may use at most 128 MiB of HBM per device.

v0:
```python
import math

import jax
import jax.numpy as jnp
import numpy as np
from jax import lax
from jax.experimental import pallas as pl
from jax.experimental.pallas import tpu as pltpu
from jax.sharding import PartitionSpec as P


spacing = 0.08
axes = ("band", "slab")
piece_bytes = 512 << 10
spare_bytes = 4 << 20


def circle_tables(count):
    quarter = count // 4
    eighth = np.sin(2.0 * np.pi * np.arange(quarter + 1) / count)
    eighth[quarter] = 1.0
    first = np.concatenate([eighth[:quarter], eighth[:0:-1]])
    sine = np.concatenate([first, -first])
    cosine = np.roll(sine, -quarter)
    return cosine, sine


def split_table(table):
    high = table.astype(jnp.bfloat16)
    low = (table - high.astype(np.float64)).astype(jnp.bfloat16)
    return high, low


def dft_tables(count):
    cosine, sine = circle_tables(count)
    phases = np.arange(count)[:, None] * np.arange(count)[None, :] % count
    return cosine[phases], sine[phases]


def line_tables(count):
    cosine, sine = dft_tables(count)
    half = count // 2
    real_rows = cosine[:half].copy()
    imag_rows = -sine[:half]
    imag_rows[0] = cosine[half]
    return real_rows, imag_rows


def split(values):
    high = values.astype(jnp.bfloat16)
    low = (values - high.astype(jnp.float32)).astype(jnp.bfloat16)
    return high, low


def dot3(left, right, dims):
    def one(a, b):
        return lax.dot_general(a, b, (dims, ((), ())), preferred_element_type=jnp.float32)

    return one(left[0], right[0]) + (one(left[1], right[0]) + one(left[0], right[1]))


plain = ((1,), (0,))
rows_rows = ((1,), (1,))


def swap_blocks(parts):
    lane = lax.broadcasted_iota(jnp.int32, parts[0].shape, len(parts[0].shape) - 1)
    axis = len(parts[0].shape) - 1
    even = (lane // 32) % 2 == 0
    low = lane < 64
    pairs = []
    for first, second in ((parts[0], parts[1]), (parts[2], parts[3])):
        pairs.append(
            (
                jnp.where(even, first, pltpu.roll(second, 32, axis)),
                jnp.where(even, pltpu.roll(first, 96, axis), second),
            )
        )
    (a0, a1), (b0, b1) = pairs
    return (
        jnp.where(low, a0, pltpu.roll(b0, 64, axis)),
        jnp.where(low, a1, pltpu.roll(b1, 64, axis)),
        jnp.where(low, pltpu.roll(a0, 64, axis), b0),
        jnp.where(low, pltpu.roll(a1, 64, axis), b1),
    )


def forward_kernel(upper_ref, lower_ref, rh_ref, rl_ref, ih_ref, il_ref, out_ref):
    rows = jnp.concatenate([half[zq] for zq in range(8) for half in (upper_ref, lower_ref)], axis=0)
    mean = jnp.sum(rows) * (1.0 / rows.size)
    operand = split(rows - mean)
    real = dot3((rh_ref[...], rl_ref[...]), operand, rows_rows)
    zero = lax.broadcasted_iota(jnp.int32, real.shape, 0) == 0
    real = real + jnp.where(zero, mean * rows.shape[1], 0.0)
    imag = dot3((ih_ref[...], il_ref[...]), operand, rows_rows)
    low = lax.broadcasted_iota(jnp.int32, (128, 128), 1) < 64
    for pair in range(4):
        a = real[:, pair * 128 : (pair + 1) * 128]
        b = imag[:, pair * 128 : (pair + 1) * 128]
        out_ref[:, 2 * pair, :] = jnp.where(low, a, pltpu.roll(b, 64, 1))
        out_ref[:, 2 * pair + 1, :] = jnp.where(low, pltpu.roll(a, 64, 1), b)


def plane_kernel(freq_ref, message_ref, ch_ref, cl_ref, sh_ref, sl_ref, out_ref):
    count = 256
    cosine = (ch_ref[...], cl_ref[...])
    sine = (sh_ref[...], sl_ref[...])
    columns = [[], []]
    for group in range(2):
        parts = [
            message_ref[(group * 4 + member) * 16 : (group * 4 + member + 1) * 16]
            for member in range(4)
        ]
        blocks = swap_blocks(parts)
        for part in range(2):
            whole = jnp.stack([blocks[part * 2], blocks[part * 2 + 1]], axis=1)
            columns[part].append(whole.reshape(count, 128))
    planes = [jnp.concatenate(columns[part], axis=1) for part in range(2)]
    means = [jnp.sum(part) * (1.0 / count**2) for part in planes]
    operand = split(jnp.concatenate([part - mean for part, mean in zip(planes, means)], axis=0))
    by_cos = dot3(operand, cosine, plain)
    by_sin = dot3(operand, sine, plain)
    real = by_cos[:count] + by_sin[count:]
    imag = by_cos[count:] - by_sin[:count]
    operand = split(jnp.concatenate([real, imag], axis=1))
    by_cos = dot3(cosine, operand, plain)
    by_sin = dot3(sine, operand, plain)
    real = by_cos[:, :count] + by_sin[:, count:]
    imag = by_cos[:, count:] - by_sin[:, :count]

    def signed(axis):
        index = lax.broadcasted_iota(jnp.int32, (count, count), axis)
        return jnp.where(index < count // 2, index, index - count).astype(jnp.float32)

    freq_z = signed(0)
    freq_x = signed(1)
    plane_sq = freq_z * freq_z + freq_x * freq_x
    zero = plane_sq == 0.0
    real = real + jnp.where(zero, means[0] * count**2, 0.0)
    imag = imag + jnp.where(zero, means[1] * count**2, 0.0)
    scale = (2.0 * math.pi / (count * spacing)) ** 2

    def green(freq_y):
        wave_sq = scale * (plane_sq + freq_y * freq_y)
        anchor = wave_sq == 0.0
        return jnp.where(
            anchor, 0.0, (4.0 * math.pi / count**3) / (wave_sq + anchor.astype(jnp.float32))
        )

    green_a = green(freq_ref[0])
    green_b = green(freq_ref[1])
    operand = split(
        jnp.concatenate([real * green_a, imag * green_a, real * green_b, imag * green_b], axis=1)
    )
    by_cos = dot3(cosine, operand, plain)
    by_sin = dot3(sine, operand, plain)
    real_a = by_cos[:, :count] - by_sin[:, count : 2 * count]
    imag_a = by_cos[:, count : 2 * count] + by_sin[:, :count]
    real_b = by_cos[:, 2 * count : 3 * count] - by_sin[:, 3 * count :]
    imag_b = by_cos[:, 3 * count :] + by_sin[:, 2 * count : 3 * count]
    result = dot3(split(jnp.concatenate([real_a, imag_b], axis=0)), cosine, plain) + dot3(
        split(jnp.concatenate([-imag_a, real_b], axis=0)), sine, plain
    )
    for group in range(2):
        blocks = []
        for part in range(2):
            whole = result[part * count : (part + 1) * count, group * 128 : (group + 1) * 128]
            whole = whole.reshape(16, 2, 8, 128)
            blocks += [whole[:, 0], whole[:, 1]]
        for member, values in enumerate(swap_blocks(blocks)):
            out_ref[(group * 4 + member) * 16 : (group * 4 + member + 1) * 16] = values


def inverse_kernel(message_ref, rh_ref, rl_ref, ih_ref, il_ref, out_ref):
    real_table = (rh_ref[...], rl_ref[...])
    imag_table = (ih_ref[...], il_ref[...])
    for zq in range(8):
        rows = message_ref[:, zq, :].T
        real = dot3(split(rows[:64]), real_table, plain)
        imag = dot3(split(rows[64:]), imag_table, plain)
        lines = real + imag
        out_ref[zq] = lines[:32]
        out_ref[zq + 8] = lines[32:]


def density_kernel(pieces, occupation_ref, orbitals_ref, *refs):
    outs, (buffer, weights_ref, sems) = refs[:-3], refs[-3:]
    flat = [piece for group in pieces for piece in group]
    copies = []
    rank = lax.axis_index("band")
    for slot, (half, dx, dz) in enumerate(flat):
        block = (rank + 4 * dz) // 4 % 2 * 4 + (rank + dx) % 4
        source = orbitals_ref.at[:, pl.ds(half * 8, 8), pl.ds(block * 32, 32), :]
        copies.append(pltpu.make_async_copy(source, buffer.at[slot], sems.at[slot]))
    weigh = pltpu.make_async_copy(occupation_ref, weights_ref, sems.at[len(flat)])
    for copy in [weigh, *copies]:
        copy.start()
    weigh.wait()
    weights = [weights_ref[band] for band in range(4)]
    slot = 0
    for out, group in zip(outs, pieces):
        for place in range(len(group)):
            copies[slot].wait()
            total = None
            for band in range(4):
                values = buffer[slot, band].astype(jnp.float32)
                term = values * values * weights[band]
                total = term if total is None else total + term
            if len(group) == 1:
                out[...] = total
            else:
                out[place] = total
            slot += 1


def partial_densities(orbitals, occupation, pieces):
    shapes = [
        pltpu.VMEM((8, 32, 256) if len(g) == 1 else (len(g), 8, 32, 256), jnp.float32)
        for g in pieces
    ]
    count = sum(len(g) for g in pieces)
    limit = count * piece_bytes * 2 + spare_bytes
    return pl.pallas_call(
        lambda *refs: density_kernel(pieces, *refs),
        out_shape=shapes,
        in_specs=[pl.BlockSpec(memory_space=pltpu.HBM)] * 2,
        out_specs=[pl.BlockSpec(memory_space=pltpu.VMEM)] * len(shapes),
        scratch_shapes=[
            pltpu.VMEM((count, 4, 8, 32, 256), jnp.bfloat16),
            pltpu.SMEM((4,), jnp.float32),
            pltpu.SemaphoreType.DMA((count + 1,)),
        ],
        compiler_params=pltpu.CompilerParams(vmem_limit_bytes=limit),
    )(*[pltpu.with_memory_space_constraint(value, pltpu.HBM) for value in (occupation, orbitals)])


def vmem_call(kernel, out_shape, limit, operands, scalars=0):
    placed = [pltpu.with_memory_space_constraint(value, pltpu.VMEM) for value in operands[scalars:]]
    vmem = pl.BlockSpec(memory_space=pltpu.VMEM)
    return pl.pallas_call(
        kernel,
        out_shape=out_shape,
        in_specs=[pl.BlockSpec(memory_space=pltpu.SMEM)] * scalars + [vmem] * len(placed),
        out_specs=jax.tree.map(lambda shape: vmem, out_shape),
        compiler_params=pltpu.CompilerParams(vmem_limit_bytes=limit),
    )(*operands[:scalars], *placed)


def solve(orbitals, occupation):
    count = orbitals.shape[2]
    half = count // 2
    upper, lower = band_sum(orbitals, occupation)

    forward_real, forward_imag = line_tables(count)
    tables = [*split_table(forward_real), *split_table(forward_imag)]
    block = jax.ShapeDtypeStruct((16, 32, count), jnp.float32)
    exchanged = pltpu.VMEM((half, 8, 128), jnp.float32)
    message = vmem_call(forward_kernel, exchanged, 12 << 20, (upper, lower, *tables))
    density = jnp.concatenate([upper, lower], axis=0)
    message = lax.all_to_all(message, axes, 0, 0, tiled=True)

    rank = lax.axis_index("band") * lax.axis_size("slab") + lax.axis_index("slab")
    freq = jnp.stack([rank, jnp.where(rank == 0, half, rank)]).astype(jnp.float32)
    cosine, sine = dft_tables(count)
    tables = [*split_table(cosine), *split_table(sine)]
    message = vmem_call(plane_kernel, exchanged, 24 << 20, (freq, message, *tables), 1)
    message = lax.all_to_all(message, axes, 0, 0, tiled=True)

    weight = np.full((half, 1), 2.0)
    weight[0] = 1.0
    tables = [*split_table(forward_real * weight), *split_table(forward_imag * weight)]
    potential = vmem_call(inverse_kernel, block, 12 << 20, (message, *tables))
    return density, potential


def ring(dx, dz):
    pairs = []
    for z in range(2):
        for x in range(4):
            for slab in range(16):
                target = (z + dz) % 2 * 4 + (x + dx) % 4
                pairs.append(((z * 4 + x) * 16 + slab, target * 16 + slab))
    return pairs


def band_sum(orbitals, occupation):
    def send(values, dx, dz):
        return lax.ppermute(values, axes, ring(dx, dz))

    far0, far1, cross0 = partial_densities(orbitals, occupation, [[(0, 2, 0)], [(0, 2, 1)], [(1, 2, 1), (1, 1, 1)]])
    far0 = send(far0, 1, 0)
    far1 = send(far1, -1, 0)
    cross0 = send(cross0, 0, 1)
    right1, left0, cross1 = partial_densities(orbitals, occupation, [[(0, 1, 1)], [(0, 3, 0)], [(1, 3, 1), (1, 0, 1)]])
    from_left1 = send(right1, 1, 0)
    from_right0 = send(left0, -1, 0)
    cross1 = send(cross1, 0, 1)
    right0, left1, own0, own1, line2, line1, line3, line0 = partial_densities(
        orbitals,
        occupation,
        [[(0, 1, 0)], [(0, 3, 1)], [(0, 0, 0)], [(0, 0, 1)], [(1, 2, 0)], [(1, 1, 0)], [(1, 3, 0)], [(1, 0, 0)]],
    )
    from_left0 = send(right0 + far0, 1, 0)
    from_right1 = send(left1 + far1, -1, 0)
    lines2 = send(line2 + cross0[0], 2, 0)
    lines1 = send(line1 + cross0[1], 1, 0)
    lines3 = send(line3 + cross1[0], -1, 0)
    other = send(own1 + from_left1 + from_right1, 0, 1)
    upper = ((own0 + from_left0) + from_right0) + other
    lower = ((line0 + cross1[1]) + lines1) + (lines2 + lines3)
    return upper, lower


def solution(mesh):
    in_specs = (P("band", "slab", None, None), P("band"))
    out_specs = (P("slab", "band", None), P("slab", "band", None))
    return jax.shard_map(solve, mesh=mesh, in_specs=in_specs, out_specs=out_specs, check_vma=False)
```

profile of v0, /device:TPU:1, one launch (start us, length us, event | category | flops | bytes accessed | tf_op | source)
XLA Modules:
  0.0 95.5 jit_solution(8578191162113301112)
XLA Ops:
  0.6 1.7 %shard_map.150 = (f32[8,32,256]{2,1,0:T(8,128)S(1)}, f32[8,32,256]{2,1,0:T(8,128)S(1)}, f32[2,8,32,256]{3,2,1,0:T(8,128)S(1)}) custom-call(f32[4]{0:T(128)} %refs_0_.5, bf16[4,16,256,256]{3,2,1,0:T(8,128)(2,1)} %refs_1_.5), custom_call_target="tpu_custom_call" | custom-call | tf_op jit(solution)/shard_map/pallas_call | solution.py:223
  2.4 4.5 %collective-permute-start.8 = (f32[2,8,32,256]{3,2,1,0:T(8,128)S(1)}, f32[2,8,32,256]{3,2,1,0:T(8,128)S(1)}, u32[]{:S(2)}, u32[]{:S(2)}) collective-permute-start(f32[2,8,32,256]{3,2,1,0:T(8,128)S(1)} %get-tuple-element.27), channel_id=1, source_target_pairs={{0,64},{1,65},{2,66},{3,67},{4,68},{5,69},{6,70},{7,71},{8,72},{9,... | collective-permute-start | bytes 1572872 | tf_op jit(solution)/shard_map/ppermute | solution.py:288
  6.9 1.7 %shard_map.151 = (f32[8,32,256]{2,1,0:T(8,128)S(1)}, f32[8,32,256]{2,1,0:T(8,128)S(1)}, f32[2,8,32,256]{3,2,1,0:T(8,128)S(1)}) custom-call(f32[4]{0:T(128)} %refs_0_.5, bf16[4,16,256,256]{3,2,1,0:T(8,128)(2,1)} %refs_1_.5), custom_call_target="tpu_custom_call" | custom-call | tf_op jit(solution)/shard_map/pallas_call | solution.py:223
  8.6 0.1 collective-permute-start.7
  8.7 2.5 %collective-permute-start.4 = (f32[8,32,256]{2,1,0:T(8,128)S(1)}, f32[8,32,256]{2,1,0:T(8,128)S(1)}, u32[]{:S(2)}, u32[]{:S(2)}) collective-permute-start(f32[8,32,256]{2,1,0:T(8,128)S(1)} %get-tuple-element.23), channel_id=1, source_target_pairs={{0,48},{1,49},{2,50},{3,51},{4,52},{5,53},{6,54},{7,55},{8,56},{9,... | collective-permute-start | bytes 786440 | tf_op jit(solution)/shard_map/ppermute | solution.py:288
  11.3 0.3 collective-permute-start
  11.5 2.4 %shard_map.149 = (f32[8,32,256]{2,1,0:T(8,128)S(1)}, f32[8,32,256]{2,1,0:T(8,128)S(1)}, f32[8,32,256]{2,1,0:T(8,128)S(1)}, f32[8,32,256]{2,1,0:T(8,128)S(1)}, f3...) custom-call(f32[4]{0:T(128)} %refs_0_.5, ...), custom_call_target="tpu_custom_call" | custom-call | tf_op jit(solution)/shard_map/pallas_call | solution.py:223
  14.0 2.0 %collective-permute-done.4 = f32[8,32,256]{2,1,0:T(8,128)S(1)} collective-permute-done((f32[8,32,256]{2,1,0:T(8,128)S(1)}, f32[8,32,256]{2,1,0:T(8,128)S(1)}, u32[]{:S(2)}, u32[]{:S(2)}) %collective-permute-start.4) | collective-permute-done | bytes 262176 | tf_op jit(solution)/shard_map/ppermute | solution.py:288
  16.0 3.5 %collective-permute-start.5 = (f32[8,32,256]{2,1,0:T(8,128)S(1)}, f32[8,32,256]{2,1,0:T(8,128)S(1)}, u32[]{:S(2)}, u32[]{:S(2)}) collective-permute-start(f32[8,32,256]{2,1,0:T(8,128)S(1)} %add.49), channel_id=1, source_target_pairs={{0,48},{1,49},{2,50},{3,51},{4,52},{5,53},{6,54},{7,55},{8,56},{9,... | collective-permute-start | bytes 786440 | tf_op jit(solution)/shard_map/ppermute | solution.py:288
  19.5 0.1 fusion.1
  19.6 1.8 %collective-permute-start.10 = (f32[8,32,256]{2,1,0:T(8,128)S(1)}, f32[8,32,256]{2,1,0:T(8,128)S(1)}, u32[]{:S(2)}, u32[]{:S(2)}) collective-permute-start(f32[8,32,256]{2,1,0:T(8,128)S(1)} %get-tuple-element.30), channel_id=1, source_target_pairs={{0,32},{1,33},{2,34},{3,35},{4,36},{5,37},{6,38},{7,39},{8,40},{9,... | collective-permute-start | bytes 786440 | tf_op jit(solution)/shard_map/ppermute | solution.py:288
  21.4 8.3 %collective-permute-done.7 = f32[2,8,32,256]{3,2,1,0:T(8,128)S(1)} collective-permute-done((f32[2,8,32,256]{3,2,1,0:T(8,128)S(1)}, f32[2,8,32,256]{3,2,1,0:T(8,128)S(1)}, u32[]{:S(2)}, u32[]{:S(2)}) %collective-permute-start.7) | collective-permute-done | bytes 524320 | tf_op jit(solution)/shard_map/ppermute | solution.py:288
  29.7 1.2 %collective-permute-start.9 = (f32[8,32,256]{2,1,0:T(8,128)S(1)}, f32[8,32,256]{2,1,0:T(8,128)S(1)}, u32[]{:S(2)}, u32[]{:S(2)}) collective-permute-start(f32[8,32,256]{2,1,0:T(8,128)S(1)} %get-tuple-element.31), channel_id=1, source_target_pairs={{0,16},{1,17},{2,18},{3,19},{4,20},{5,21},{6,22},{7,23},{8,24},{9,... | collective-permute-start | bytes 786440 | tf_op jit(solution)/shard_map/ppermute | solution.py:288
  31.0 1.5 %collective-permute-start.11 = (f32[8,32,256]{2,1,0:T(8,128)S(1)}, f32[8,32,256]{2,1,0:T(8,128)S(1)}, u32[]{:S(2)}, u32[]{:S(2)}) collective-permute-start(f32[8,32,256]{2,1,0:T(8,128)S(1)} %fusion), channel_id=1, source_target_pairs={{0,48},{1,49},{2,50},{3,51},{4,52},{5,53},{6,54},{7,55},{8,56},{9,... | collective-permute-start | bytes 786440 | tf_op jit(solution)/shard_map/ppermute | solution.py:288
  32.6 1.3 %collective-permute-start.2 = (f32[8,32,256]{2,1,0:T(8,128)S(1)}, f32[8,32,256]{2,1,0:T(8,128)S(1)}, u32[]{:S(2)}, u32[]{:S(2)}) collective-permute-start(f32[8,32,256]{2,1,0:T(8,128)S(1)} %get-tuple-element.19), channel_id=1, source_target_pairs={{0,48},{1,49},{2,50},{3,51},{4,52},{5,53},{6,54},{7,55},{8,56},{9,... | collective-permute-start | bytes 786440 | tf_op jit(solution)/shard_map/ppermute | solution.py:288
  33.9 0.2 collective-permute-start.1
  34.1 0.1 add_add_fusion
  34.2 2.8 %collective-permute-start.6 = (f32[8,32,256]{2,1,0:T(8,128)S(1)}, f32[8,32,256]{2,1,0:T(8,128)S(1)}, u32[]{:S(2)}, u32[]{:S(2)}) collective-permute-start(f32[8,32,256]{2,1,0:T(8,128)S(1)} %add_add_fusion), channel_id=1, source_target_pairs={{0,64},{1,65},{2,66},{3,67},{4,68},{5,69},{6,70},{7,71},{8,72},{9,... | collective-permute-start | bytes 786440 | tf_op jit(solution)/shard_map/ppermute | solution.py:288
  36.9 0.6 collective-permute-done.9
  37.6 0.1 fusion.5.lower_ref
  37.6 5.4 %collective-permute-done.2 = f32[8,32,256]{2,1,0:T(8,128)S(1)} collective-permute-done((f32[8,32,256]{2,1,0:T(8,128)S(1)}, f32[8,32,256]{2,1,0:T(8,128)S(1)}, u32[]{:S(2)}, u32[]{:S(2)}) %collective-permute-start.2) | collective-permute-done | bytes 262176 | tf_op jit(solution)/shard_map/ppermute | solution.py:288
  43.0 0.4 collective-permute-done.1
  43.4 0.1 add_add_fusion.1.upper_ref
  43.6 2.0 %shard_map.152 = f32[128,8,128]{2,1,0:T(8,128)} custom-call(f32[8,32,256]{2,1,0:T(8,128)S(1)} %add_add_fusion.1.upper_ref, f32[8,32,256]{2,1,0:T(8,128)S(1)} %fusion.5.lower_ref, bf16[128,256]{1,0:T(8,128)(2,1)S(1)} %copy-done.8, bf16[128,256]{1,0:T(8,128)(2,1)S(1)} %copy-done.9, bf16[128,256]{1,0:T(8,128)(2,1)S(1)} %copy-done.10, ...), custom_call_target="tpu_custom_call" | custom-call | tf_op jit(solution)/shard_map/pallas_call | solution.py:240
  45.5 11.0 %all-to-all-start = ((f32[128,8,128]{2,1,0:T(8,128)}), f32[128,8,128]{2,1,0:T(8,128)S(1)}, u32[]{:S(2)}, u32[]{:S(2)}) async-start(f32[128,8,128]{2,1,0:T(8,128)} %shard_map.152), calls=%async_computation | async-start | bytes 1048576 | tf_op jit(solution)/shard_map/all_to_all | solution.py:260
  56.5 0.1 add_convert_fusion.freq_ref
  56.6 14.0 %all-to-all-done.message_ref = f32[128,8,128]{2,1,0:T(8,128)S(1)} async-done(((f32[128,8,128]{2,1,0:T(8,128)}), f32[128,8,128]{2,1,0:T(8,128)S(1)}, u32[]{:S(2)}, u32[]{:S(2)}) %all-to-all-start) | async-done | bytes 524320 | tf_op jit(solution)/shard_map/all_to_all | solution.py:260
  70.6 5.4 %shard_map.153 = f32[128,8,128]{2,1,0:T(8,128)} custom-call(f32[2]{0:T(128)S(1)} %add_convert_fusion.freq_ref, f32[128,8,128]{2,1,0:T(8,128)S(1)} %all-to-all-done.message_ref, bf16[256,256]{1,0:T(8,128)(2,1)S(1)} %copy-done, bf16[256,256]{1,0:T(8,128)(2,1)S(1)} %copy-done.1, bf16[256,256]{1,0:T(8,128)(2,1)S(1)} %copy-done.2, bf16[256,256]{1,0:T(8,128)(2,1)S(1)} %copy-done.3), custom_call_target="tpu_custom_call" | custom-call | tf_op jit(solution)/shard_map/pallas_call | solution.py:240
  76.0 3.9 %all-to-all-start.1 = ((f32[128,8,128]{2,1,0:T(8,128)}), f32[128,8,128]{2,1,0:T(8,128)S(1)}, u32[]{:S(2)}, u32[]{:S(2)}) async-start(f32[128,8,128]{2,1,0:T(8,128)} %shard_map.153), calls=%async_computation.1 | async-start | bytes 1048576 | tf_op jit(solution)/shard_map/all_to_all | solution.py:267
  79.9 0.8 pad_maximum_fusion
  80.7 13.3 %all-to-all-done.1.message_ref = f32[128,8,128]{2,1,0:T(8,128)S(1)} async-done(((f32[128,8,128]{2,1,0:T(8,128)}), f32[128,8,128]{2,1,0:T(8,128)S(1)}, u32[]{:S(2)}, u32[]{:S(2)}) %all-to-all-start.1) | async-done | bytes 524320 | tf_op jit(solution)/shard_map/all_to_all | solution.py:267
  94.0 1.5 %shard_map.154 = f32[16,32,256]{2,1,0:T(8,128)} custom-call(f32[128,8,128]{2,1,0:T(8,128)S(1)} %all-to-all-done.1.message_ref, bf16[128,256]{1,0:T(8,128)(2,1)S(1)} %copy-done.4, bf16[128,256]{1,0:T(8,128)(2,1)S(1)} %copy-done.5, bf16[128,256]{1,0:T(8,128)(2,1)S(1)} %copy-done.6, bf16[128,256]{1,0:T(8,128)(2,1)S(1)} %copy-done.7), custom_call_target="tpu_custom_call" | custom-call | tf_op jit(solution)/shard_map/pallas_call | solution.py:240
  (35 shorter events, 0.2 us)
Async XLA Ops:
  2.4 17.1 %collective-permute-start.8 = (f32[2,8,32,256]{3,2,1,0:T(8,128)S(1)}, f32[2,8,32,256]{3,2,1,0:T(8,128)S(1)}, u32[]{:S(2)}, u32[]{:S(2)}) collective-permute-start(f32[2,8,32,256]{3,2,1,0:T(8,128)S(1)} %get-tuple-element.27), channel_id=1, source_target_pairs={{0,64},{1,65},{2,66},{3,67},{4,68},{5,69},{6,70},{7,71},{8,72},{9,... | collective-permute-start | bytes 1572872 | tf_op jit(solution)/shard_map/ppermute | solution.py:288
  8.6 35.0 %copy-start.8 = (bf16[128,256]{1,0:T(8,128)(2,1)S(1)}, bf16[128,256]{1,0:T(8,128)(2,1)}, u32[]{:S(2)}) copy-start(bf16[128,256]{1,0:T(8,128)(2,1)} %constant.39.clone.rh_ref) | copy-start | bytes 196612
  8.6 35.0 %copy-start.9 = (bf16[128,256]{1,0:T(8,128)(2,1)S(1)}, bf16[128,256]{1,0:T(8,128)(2,1)}, u32[]{:S(2)}) copy-start(bf16[128,256]{1,0:T(8,128)(2,1)} %constant.40.clone.rl_ref) | copy-start | bytes 196612
  8.6 34.9 %copy-start.10 = (bf16[128,256]{1,0:T(8,128)(2,1)S(1)}, bf16[128,256]{1,0:T(8,128)(2,1)}, u32[]{:S(2)}) copy-start(bf16[128,256]{1,0:T(8,128)(2,1)} %constant.41.clone.ih_ref) | copy-start | bytes 196612
  8.6 34.9 %copy-start.11 = (bf16[128,256]{1,0:T(8,128)(2,1)S(1)}, bf16[128,256]{1,0:T(8,128)(2,1)}, u32[]{:S(2)}) copy-start(bf16[128,256]{1,0:T(8,128)(2,1)} %constant.42.clone.il_ref) | copy-start | bytes 196612
  8.6 21.1 %collective-permute-start.7 = (f32[2,8,32,256]{3,2,1,0:T(8,128)S(1)}, f32[2,8,32,256]{3,2,1,0:T(8,128)S(1)}, u32[]{:S(2)}, u32[]{:S(2)}) collective-permute-start(f32[2,8,32,256]{3,2,1,0:T(8,128)S(1)} %get-tuple-element.25), channel_id=1, source_target_pairs={{0,64},{1,65},{2,66},{3,67},{4,68},{5,69},{6,70},{7,71},{8,72},{9,... | collective-permute-start | bytes 1572872 | tf_op jit(solution)/shard_map/ppermute | solution.py:288
  8.7 7.2 %collective-permute-start.4 = (f32[8,32,256]{2,1,0:T(8,128)S(1)}, f32[8,32,256]{2,1,0:T(8,128)S(1)}, u32[]{:S(2)}, u32[]{:S(2)}) collective-permute-start(f32[8,32,256]{2,1,0:T(8,128)S(1)} %get-tuple-element.23), channel_id=1, source_target_pairs={{0,48},{1,49},{2,50},{3,51},{4,52},{5,53},{6,54},{7,55},{8,56},{9,... | collective-permute-start | bytes 786440 | tf_op jit(solution)/shard_map/ppermute | solution.py:288
  11.3 21.3 %collective-permute-start.3 = (f32[8,32,256]{2,1,0:T(8,128)S(1)}, f32[8,32,256]{2,1,0:T(8,128)S(1)}, u32[]{:S(2)}, u32[]{:S(2)}) collective-permute-start(f32[8,32,256]{2,1,0:T(8,128)S(1)} %get-tuple-element.21), channel_id=1, source_target_pairs={{0,16},{1,17},{2,18},{3,19},{4,20},{5,21},{6,22},{7,23},{8,24},{9,... | collective-permute-start | bytes 786440 | tf_op jit(solution)/shard_map/ppermute | solution.py:288
  11.3 59.3 %copy-start = (bf16[256,256]{1,0:T(8,128)(2,1)S(1)}, bf16[256,256]{1,0:T(8,128)(2,1)}, u32[]{:S(2)}) copy-start(bf16[256,256]{1,0:T(8,128)(2,1)} %constant.43.clone.ch_ref) | copy-start | bytes 393220
  11.3 59.3 %copy-start.1 = (bf16[256,256]{1,0:T(8,128)(2,1)S(1)}, bf16[256,256]{1,0:T(8,128)(2,1)}, u32[]{:S(2)}) copy-start(bf16[256,256]{1,0:T(8,128)(2,1)} %constant.44.clone.cl_ref) | copy-start | bytes 393220
  11.3 59.3 %copy-start.2 = (bf16[256,256]{1,0:T(8,128)(2,1)S(1)}, bf16[256,256]{1,0:T(8,128)(2,1)}, u32[]{:S(2)}) copy-start(bf16[256,256]{1,0:T(8,128)(2,1)} %constant.45.clone.sh_ref) | copy-start | bytes 393220
  11.3 59.3 %copy-start.3 = (bf16[256,256]{1,0:T(8,128)(2,1)S(1)}, bf16[256,256]{1,0:T(8,128)(2,1)}, u32[]{:S(2)}) copy-start(bf16[256,256]{1,0:T(8,128)(2,1)} %constant.46.clone.sl_ref) | copy-start | bytes 393220
  11.3 19.7 %collective-permute-start = (f32[8,32,256]{2,1,0:T(8,128)S(1)}, f32[8,32,256]{2,1,0:T(8,128)S(1)}, u32[]{:S(2)}, u32[]{:S(2)}) collective-permute-start(f32[8,32,256]{2,1,0:T(8,128)S(1)} %get-tuple-element.18), channel_id=1, source_target_pairs={{0,16},{1,17},{2,18},{3,19},{4,20},{5,21},{6,22},{7,23},{8,24},{9,... | collective-permute-start | bytes 786440 | tf_op jit(solution)/shard_map/ppermute | solution.py:288
  13.9 80.1 %copy-start.4 = (bf16[128,256]{1,0:T(8,128)(2,1)S(1)}, bf16[128,256]{1,0:T(8,128)(2,1)}, u32[]{:S(2)}) copy-start(bf16[128,256]{1,0:T(8,128)(2,1)} %constant.47.clone.rh_ref) | copy-start | bytes 196612
  13.9 80.1 %copy-start.5 = (bf16[128,256]{1,0:T(8,128)(2,1)S(1)}, bf16[128,256]{1,0:T(8,128)(2,1)}, u32[]{:S(2)}) copy-start(bf16[128,256]{1,0:T(8,128)(2,1)} %constant.48.clone.rl_ref) | copy-start | bytes 196612
  13.9 80.1 %copy-start.6 = (bf16[128,256]{1,0:T(8,128)(2,1)S(1)}, bf16[128,256]{1,0:T(8,128)(2,1)}, u32[]{:S(2)}) copy-start(bf16[128,256]{1,0:T(8,128)(2,1)} %constant.49.clone.ih_ref) | copy-start | bytes 196612
  14.0 80.1 %copy-start.7 = (bf16[128,256]{1,0:T(8,128)(2,1)S(1)}, bf16[128,256]{1,0:T(8,128)(2,1)}, u32[]{:S(2)}) copy-start(bf16[128,256]{1,0:T(8,128)(2,1)} %constant.50.clone.il_ref) | copy-start | bytes 196612
  16.0 17.9 %collective-permute-start.5 = (f32[8,32,256]{2,1,0:T(8,128)S(1)}, f32[8,32,256]{2,1,0:T(8,128)S(1)}, u32[]{:S(2)}, u32[]{:S(2)}) collective-permute-start(f32[8,32,256]{2,1,0:T(8,128)S(1)} %add.49), channel_id=1, source_target_pairs={{0,48},{1,49},{2,50},{3,51},{4,52},{5,53},{6,54},{7,55},{8,56},{9,... | collective-permute-start | bytes 786440 | tf_op jit(solution)/shard_map/ppermute | solution.py:288
  19.6 14.6 %collective-permute-start.10 = (f32[8,32,256]{2,1,0:T(8,128)S(1)}, f32[8,32,256]{2,1,0:T(8,128)S(1)}, u32[]{:S(2)}, u32[]{:S(2)}) collective-permute-start(f32[8,32,256]{2,1,0:T(8,128)S(1)} %get-tuple-element.30), channel_id=1, source_target_pairs={{0,32},{1,33},{2,34},{3,35},{4,36},{5,37},{6,38},{7,39},{8,40},{9,... | collective-permute-start | bytes 786440 | tf_op jit(solution)/shard_map/ppermute | solution.py:288
  29.7 7.8 %collective-permute-start.9 = (f32[8,32,256]{2,1,0:T(8,128)S(1)}, f32[8,32,256]{2,1,0:T(8,128)S(1)}, u32[]{:S(2)}, u32[]{:S(2)}) collective-permute-start(f32[8,32,256]{2,1,0:T(8,128)S(1)} %get-tuple-element.31), channel_id=1, source_target_pairs={{0,16},{1,17},{2,18},{3,19},{4,20},{5,21},{6,22},{7,23},{8,24},{9,... | collective-permute-start | bytes 786440 | tf_op jit(solution)/shard_map/ppermute | solution.py:288
  31.0 6.6 %collective-permute-start.11 = (f32[8,32,256]{2,1,0:T(8,128)S(1)}, f32[8,32,256]{2,1,0:T(8,128)S(1)}, u32[]{:S(2)}, u32[]{:S(2)}) collective-permute-start(f32[8,32,256]{2,1,0:T(8,128)S(1)} %fusion), channel_id=1, source_target_pairs={{0,48},{1,49},{2,50},{3,51},{4,52},{5,53},{6,54},{7,55},{8,56},{9,... | collective-permute-start | bytes 786440 | tf_op jit(solution)/shard_map/ppermute | solution.py:288
  32.6 10.4 %collective-permute-start.2 = (f32[8,32,256]{2,1,0:T(8,128)S(1)}, f32[8,32,256]{2,1,0:T(8,128)S(1)}, u32[]{:S(2)}, u32[]{:S(2)}) collective-permute-start(f32[8,32,256]{2,1,0:T(8,128)S(1)} %get-tuple-element.19), channel_id=1, source_target_pairs={{0,48},{1,49},{2,50},{3,51},{4,52},{5,53},{6,54},{7,55},{8,56},{9,... | collective-permute-start | bytes 786440 | tf_op jit(solution)/shard_map/ppermute | solution.py:288
  33.9 9.5 %collective-permute-start.1 = (f32[8,32,256]{2,1,0:T(8,128)S(1)}, f32[8,32,256]{2,1,0:T(8,128)S(1)}, u32[]{:S(2)}, u32[]{:S(2)}) collective-permute-start(f32[8,32,256]{2,1,0:T(8,128)S(1)} %add.45), channel_id=1, source_target_pairs={{0,16},{1,17},{2,18},{3,19},{4,20},{5,21},{6,22},{7,23},{8,24},{9,... | collective-permute-start | bytes 786440 | tf_op jit(solution)/shard_map/ppermute | solution.py:288
  34.2 9.3 %collective-permute-start.6 = (f32[8,32,256]{2,1,0:T(8,128)S(1)}, f32[8,32,256]{2,1,0:T(8,128)S(1)}, u32[]{:S(2)}, u32[]{:S(2)}) collective-permute-start(f32[8,32,256]{2,1,0:T(8,128)S(1)} %add_add_fusion), channel_id=1, source_target_pairs={{0,64},{1,65},{2,66},{3,67},{4,68},{5,69},{6,70},{7,71},{8,72},{9,... | collective-permute-start | bytes 786440 | tf_op jit(solution)/shard_map/ppermute | solution.py:288
  45.5 25.1 %all-to-all-start = ((f32[128,8,128]{2,1,0:T(8,128)}), f32[128,8,128]{2,1,0:T(8,128)S(1)}, u32[]{:S(2)}, u32[]{:S(2)}) async-start(f32[128,8,128]{2,1,0:T(8,128)} %shard_map.152), calls=%async_computation | async-start | bytes 1048576 | tf_op jit(solution)/shard_map/all_to_all | solution.py:260
  76.0 18.0 %all-to-all-start.1 = ((f32[128,8,128]{2,1,0:T(8,128)}), f32[128,8,128]{2,1,0:T(8,128)S(1)}, u32[]{:S(2)}, u32[]{:S(2)}) async-start(f32[128,8,128]{2,1,0:T(8,128)} %shard_map.153), calls=%async_computation.1 | async-start | bytes 1048576 | tf_op jit(solution)/shard_map/all_to_all | solution.py:267
where the time goes:
time: 95.8 us; the launch traced here: 95.5 us
  waiting for transfers between devices  44 us (46%)
  starting transfers between devices  34.6 us (36%)
  Pallas kernels  14.6 us (15%)
  other arithmetic  1.31 us (1%)
    all_to_all x2, waiting for transfers between devices, solve(): message = lax.all_to_all(message, axes, 0, 0, tiled=True)  27.3 us
    ppermute x12, starting transfers between devices, send(): return lax.ppermute(values, axes, ring(dx, dz))  19.7 us
    ppermute x12, waiting for transfers between devices, send(): return lax.ppermute(values, axes, ring(dx, dz))  16.8 us
    all_to_all x2, starting transfers between devices, solve(): message = lax.all_to_all(message, axes, 0, 0, tiled=True)  14.9 us
    pallas_call x3, Pallas kernels, vmem_call(): pl.pallas_call(kernel, out_shape=out_shape, in_specs=[pl.BlockSpec(memory...  8.8 us
    pallas_call x3, Pallas kernels, partial_densities(): pl.pallas_call(lambda *refs: density_kernel(pieces, *refs), out_shape=sha...  5.8 us
  transfers between devices with their start and end apart: 14, of which 7 were waited for; matrix products, arithmetic and copies ran while one was open for 1% of the time, Pallas kernels for 4%

commit v1 on v0

--- a/solution.py
+++ b/solution.py
@@ -53,10 +53,11 @@
 
 
 def dot3(left, right, dims):
-    def one(a, b):
-        return lax.dot_general(a, b, (dims, ((), ())), preferred_element_type=jnp.float32)
-
-    return one(left[0], right[0]) + (one(left[1], right[0]) + one(left[0], right[1]))
+    first = jnp.concatenate([left[0], left[1], left[0]], axis=dims[0][0])
+    second = jnp.concatenate([right[0], right[0], right[1]], axis=dims[1][0])
+    return lax.dot_general(
+        first, second, (dims, ((), ())), preferred_element_type=jnp.float32
+    )
 
 
 plain = ((1,), (0,))
@@ -85,14 +86,13 @@
     )
 
 
-def forward_kernel(upper_ref, lower_ref, rh_ref, rl_ref, ih_ref, il_ref, out_ref):
+def forward_kernel(upper_ref, lower_ref, high_ref, low_ref, out_ref):
     rows = jnp.concatenate([half[zq] for zq in range(8) for half in (upper_ref, lower_ref)], axis=0)
     mean = jnp.sum(rows) * (1.0 / rows.size)
-    operand = split(rows - mean)
-    real = dot3((rh_ref[...], rl_ref[...]), operand, rows_rows)
-    zero = lax.broadcasted_iota(jnp.int32, real.shape, 0) == 0
-    real = real + jnp.where(zero, mean * rows.shape[1], 0.0)
-    imag = dot3((ih_ref[...], il_ref[...]), operand, rows_rows)
+    lines = dot3((high_ref[...], low_ref[...]), split(rows - mean), rows_rows)
+    zero = lax.broadcasted_iota(jnp.int32, (128, 512), 0) == 0
+    real = lines[:128] + jnp.where(zero, mean * rows.shape[1], 0.0)
+    imag = lines[128:]
     low = lax.broadcasted_iota(jnp.int32, (128, 128), 1) < 64
     for pair in range(4):
         a = real[:, pair * 128 : (pair + 1) * 128]
@@ -101,10 +101,10 @@
         out_ref[:, 2 * pair + 1, :] = jnp.where(low, pltpu.roll(a, 64, 1), b)
 
 
-def plane_kernel(freq_ref, message_ref, ch_ref, cl_ref, sh_ref, sl_ref, out_ref):
+def plane_kernel(freq_ref, message_ref, high_ref, low_ref, out_ref):
     count = 256
-    cosine = (ch_ref[...], cl_ref[...])
-    sine = (sh_ref[...], sl_ref[...])
+    stacked = (high_ref[...], low_ref[...])
+    beside = [jnp.concatenate([table[:count], table[count:]], axis=1) for table in stacked]
     columns = [[], []]
     for group in range(2):
         parts = [
@@ -118,13 +118,13 @@
     planes = [jnp.concatenate(columns[part], axis=1) for part in range(2)]
     means = [jnp.sum(part) * (1.0 / count**2) for part in planes]
     operand = split(jnp.concatenate([part - mean for part, mean in zip(planes, means)], axis=0))
-    by_cos = dot3(operand, cosine, plain)
-    by_sin = dot3(operand, sine, plain)
+    both = dot3(operand, beside, plain)
+    by_cos, by_sin = both[:, :count], both[:, count:]
     real = by_cos[:count] + by_sin[count:]
     imag = by_cos[count:] - by_sin[:count]
     operand = split(jnp.concatenate([real, imag], axis=1))
-    by_cos = dot3(cosine, operand, plain)
-    by_sin = dot3(sine, operand, plain)
+    both = dot3(stacked, operand, plain)
+    by_cos, by_sin = both[:count], both[count:]
     real = by_cos[:, :count] + by_sin[:, count:]
     imag = by_cos[:, count:] - by_sin[:, :count]
 
@@ -152,15 +152,20 @@
     operand = split(
         jnp.concatenate([real * green_a, imag * green_a, real * green_b, imag * green_b], axis=1)
     )
-    by_cos = dot3(cosine, operand, plain)
-    by_sin = dot3(sine, operand, plain)
+    both = dot3(stacked, operand, plain)
+    by_cos, by_sin = both[:count], both[count:]
     real_a = by_cos[:, :count] - by_sin[:, count : 2 * count]
     imag_a = by_cos[:, count : 2 * count] + by_sin[:, :count]
     real_b = by_cos[:, 2 * count : 3 * count] - by_sin[:, 3 * count :]
     imag_b = by_cos[:, 3 * count :] + by_sin[:, 2 * count : 3 * count]
-    result = dot3(split(jnp.concatenate([real_a, imag_b], axis=0)), cosine, plain) + dot3(
-        split(jnp.concatenate([-imag_a, real_b], axis=0)), sine, plain
-    )
+    pair = jnp.concatenate(
+        [
+            jnp.concatenate([real_a, -imag_a], axis=1),
+            jnp.concatenate([imag_b, real_b], axis=1),
+        ],
+        axis=0,
+    )
+    result = dot3(split(pair), stacked, plain)
     for group in range(2):
         blocks = []
         for part in range(2):
@@ -171,16 +176,16 @@
             out_ref[(group * 4 + member) * 16 : (group * 4 + member + 1) * 16] = values
 
 
-def inverse_kernel(message_ref, rh_ref, rl_ref, ih_ref, il_ref, out_ref):
-    real_table = (rh_ref[...], rl_ref[...])
-    imag_table = (ih_ref[...], il_ref[...])
+def inverse_kernel(message_ref, high_ref, low_ref, out_ref):
+    turned = [message_ref[:, zq, :].T for zq in range(8)]
+    rows = jnp.concatenate(
+        [jnp.concatenate([block[:64] for block in turned], axis=0),
+         jnp.concatenate([block[64:] for block in turned], axis=0)], axis=1
+    )
+    lines = dot3(split(rows), (high_ref[...], low_ref[...]), plain)
     for zq in range(8):
-        rows = message_ref[:, zq, :].T
-        real = dot3(split(rows[:64]), real_table, plain)
-        imag = dot3(split(rows[64:]), imag_table, plain)
-        lines = real + imag
-        out_ref[zq] = lines[:32]
-        out_ref[zq + 8] = lines[32:]
+        out_ref[zq] = lines[zq * 64 : zq * 64 + 32]
+        out_ref[zq + 8] = lines[zq * 64 + 32 : zq * 64 + 64]
 
 
 def density_kernel(pieces, occupation_ref, orbitals_ref, *refs):
@@ -252,7 +257,7 @@
     upper, lower = band_sum(orbitals, occupation)
 
     forward_real, forward_imag = line_tables(count)
-    tables = [*split_table(forward_real), *split_table(forward_imag)]
+    tables = split_table(np.concatenate([forward_real, forward_imag]))
     block = jax.ShapeDtypeStruct((16, 32, count), jnp.float32)
     exchanged = pltpu.VMEM((half, 8, 128), jnp.float32)
     message = vmem_call(forward_kernel, exchanged, 12 << 20, (upper, lower, *tables))
@@ -262,13 +267,13 @@
     rank = lax.axis_index("band") * lax.axis_size("slab") + lax.axis_index("slab")
     freq = jnp.stack([rank, jnp.where(rank == 0, half, rank)]).astype(jnp.float32)
     cosine, sine = dft_tables(count)
-    tables = [*split_table(cosine), *split_table(sine)]
+    tables = split_table(np.concatenate([cosine, sine]))
     message = vmem_call(plane_kernel, exchanged, 24 << 20, (freq, message, *tables), 1)
     message = lax.all_to_all(message, axes, 0, 0, tiled=True)
 
     weight = np.full((half, 1), 2.0)
     weight[0] = 1.0
-    tables = [*split_table(forward_real * weight), *split_table(forward_imag * weight)]
+    tables = split_table(np.concatenate([forward_real * weight, forward_imag * weight]))
     potential = vmem_call(inverse_kernel, block, 12 << 20, (message, *tables))
     return density, potential
 
@@ -302,12 +307,16 @@
     )
     from_left0 = send(right0 + far0, 1, 0)
     from_right1 = send(left1 + far1, -1, 0)
-    lines2 = send(line2 + cross0[0], 2, 0)
-    lines1 = send(line1 + cross0[1], 1, 0)
-    lines3 = send(line3 + cross1[0], -1, 0)
+    line2 = line2 + cross0[0]
+    ahead = send(line2[:4], 1, 0)
+    behind = send(line2[4:], -1, 0)
+    line1 = line1 + cross0[1]
+    lines1 = send(lax.dynamic_update_slice(line1, line1[:4] + ahead, (0, 0, 0)), 1, 0)
+    line3 = line3 + cross1[0]
+    lines3 = send(lax.dynamic_update_slice(line3, line3[4:] + behind, (4, 0, 0)), -1, 0)
     other = send(own1 + from_left1 + from_right1, 0, 1)
     upper = ((own0 + from_left0) + from_right0) + other
-    lower = ((line0 + cross1[1]) + lines1) + (lines2 + lines3)
+    lower = (line0 + cross1[1]) + (lines1 + lines3)
     return upper, lower
 
 

time: 95.8 us -> 93.6 us (0.977)
  waiting for transfers between devices: 44 us -> 39 us
  starting transfers between devices: 34.6 us -> 37.8 us
    ppermute x12 -> x13, waiting for transfers between devices: 16.8 us -> 11.7 us  [send(): return lax.ppermute(values, axes, ring(dx, dz))]
    all_to_all x2, starting transfers between devices: 14.9 us -> 16.9 us  [solve(): message = lax.all_to_all(message, axes, 0, 0, tiled=True)]
    ppermute x12 -> x13, starting transfers between devices: 19.7 us -> 20.9 us  [send(): return lax.ppermute(values, axes, ring(dx, dz))]
  transfers between devices with their start and end apart: 14 -> 15, of which waited for: 7 -> 9; matrix products, arithmetic and copies ran while one was open for 1% -> 1% of each run, Pallas kernels for 4% -> 4%
where the time goes in v1:
time: 93.6 us; the launch traced here: 93.3 us
  waiting for transfers between devices  39 us (42%)
  starting transfers between devices  37.8 us (40%)
  Pallas kernels  14.4 us (15%)
  other arithmetic  1.36 us (1%)
    all_to_all x2, waiting for transfers between devices, solve(): message = lax.all_to_all(message, axes, 0, 0, tiled=True)  27.3 us
    ppermute x13, starting transfers between devices, send(): return lax.ppermute(values, axes, ring(dx, dz))  20.9 us
    all_to_all x2, starting transfers between devices, solve(): message = lax.all_to_all(message, axes, 0, 0, tiled=True)  16.9 us
    ppermute x13, waiting for transfers between devices, send(): return lax.ppermute(values, axes, ring(dx, dz))  11.7 us
    pallas_call x3, Pallas kernels, vmem_call(): pl.pallas_call(kernel, out_shape=out_shape, in_specs=[pl.BlockSpec(memory...  8.54 us
    pallas_call x3, Pallas kernels, partial_densities(): pl.pallas_call(lambda *refs: density_kernel(pieces, *refs), out_shape=sha...  5.83 us
  transfers between devices with their start and end apart: 15, of which 9 were waited for; matrix products, arithmetic and copies ran while one was open for 1% of the time, Pallas kernels for 4%

profile of v1, /device:TPU:1, one launch (start us, length us, event | category | flops | bytes accessed | tf_op | source)
XLA Modules:
  0.0 93.3 jit_solution(10235666551611671866)
XLA Ops:
  0.6 1.7 %shard_map.96 = (f32[8,32,256]{2,1,0:T(8,128)S(1)}, f32[8,32,256]{2,1,0:T(8,128)S(1)}, f32[2,8,32,256]{3,2,1,0:T(8,128)S(1)}) custom-call(f32[4]{0:T(128)} %refs_0_.5, bf16[4,16,256,256]{3,2,1,0:T(8,128)(2,1)} %refs_1_.5), custom_call_target="tpu_custom_call" | custom-call | tf_op jit(solution)/shard_map/pallas_call | solution.py:228
  2.4 4.5 %collective-permute-start.8 = (f32[2,8,32,256]{3,2,1,0:T(8,128)S(1)}, f32[2,8,32,256]{3,2,1,0:T(8,128)S(1)}, u32[]{:S(2)}, u32[]{:S(2)}) collective-permute-start(f32[2,8,32,256]{3,2,1,0:T(8,128)S(1)} %get-tuple-element.27), channel_id=1, source_target_pairs={{0,64},{1,65},{2,66},{3,67},{4,68},{5,69},{6,70},{7,71},{8,72},{9,... | collective-permute-start | bytes 1572872 | tf_op jit(solution)/shard_map/ppermute | solution.py:293
  6.9 2.5 %collective-permute-start.4 = (f32[8,32,256]{2,1,0:T(8,128)S(1)}, f32[8,32,256]{2,1,0:T(8,128)S(1)}, u32[]{:S(2)}, u32[]{:S(2)}) collective-permute-start(f32[8,32,256]{2,1,0:T(8,128)S(1)} %get-tuple-element.23), channel_id=1, source_target_pairs={{0,48},{1,49},{2,50},{3,51},{4,52},{5,53},{6,54},{7,55},{8,56},{9,... | collective-permute-start | bytes 786440 | tf_op jit(solution)/shard_map/ppermute | solution.py:293
  9.3 1.7 %shard_map.97 = (f32[8,32,256]{2,1,0:T(8,128)S(1)}, f32[8,32,256]{2,1,0:T(8,128)S(1)}, f32[2,8,32,256]{3,2,1,0:T(8,128)S(1)}) custom-call(f32[4]{0:T(128)} %refs_0_.5, bf16[4,16,256,256]{3,2,1,0:T(8,128)(2,1)} %refs_1_.5), custom_call_target="tpu_custom_call" | custom-call | tf_op jit(solution)/shard_map/pallas_call | solution.py:228
  11.0 0.2 collective-permute-start.7
  11.2 0.3 collective-permute-start.3
  11.5 2.4 %shard_map.95 = (f32[8,32,256]{2,1,0:T(8,128)S(1)}, f32[8,32,256]{2,1,0:T(8,128)S(1)}, f32[8,32,256]{2,1,0:T(8,128)S(1)}, f32[8,32,256]{2,1,0:T(8,128)S(1)}, f32...) custom-call(f32[4]{0:T(128)} %refs_0_.5, ...), custom_call_target="tpu_custom_call" | custom-call | tf_op jit(solution)/shard_map/pallas_call | solution.py:228
  13.9 0.1 collective-permute-done.4
  14.1 3.4 %collective-permute-start.2 = (f32[8,32,256]{2,1,0:T(8,128)S(1)}, f32[8,32,256]{2,1,0:T(8,128)S(1)}, u32[]{:S(2)}, u32[]{:S(2)}) collective-permute-start(f32[8,32,256]{2,1,0:T(8,128)S(1)} %get-tuple-element.19), channel_id=1, source_target_pairs={{0,48},{1,49},{2,50},{3,51},{4,52},{5,53},{6,54},{7,55},{8,56},{9,... | collective-permute-start | bytes 786440 | tf_op jit(solution)/shard_map/ppermute | solution.py:293
  17.5 0.5 collective-permute-start.5
  18.1 0.4 collective-permute-done.8
  18.5 1.2 %collective-permute-start.1 = (f32[8,32,256]{2,1,0:T(8,128)S(1)}, f32[8,32,256]{2,1,0:T(8,128)S(1)}, u32[]{:S(2)}, u32[]{:S(2)}) collective-permute-start(f32[8,32,256]{2,1,0:T(8,128)S(1)} %add.48), channel_id=1, source_target_pairs={{0,16},{1,17},{2,18},{3,19},{4,20},{5,21},{6,22},{7,23},{8,24},{9,... | collective-permute-start | bytes 786440 | tf_op jit(solution)/shard_map/ppermute | solution.py:293
  19.7 0.1 fusion.1
  19.8 3.0 %collective-permute-done.3 = f32[8,32,256]{2,1,0:T(8,128)S(1)} collective-permute-done((f32[8,32,256]{2,1,0:T(8,128)S(1)}, f32[8,32,256]{2,1,0:T(8,128)S(1)}, u32[]{:S(2)}, u32[]{:S(2)}) %collective-permute-start.3) | collective-permute-done | bytes 262176 | tf_op jit(solution)/shard_map/ppermute | solution.py:293
  22.8 4.1 %collective-permute-done.5 = f32[8,32,256]{2,1,0:T(8,128)S(1)} collective-permute-done((f32[8,32,256]{2,1,0:T(8,128)S(1)}, f32[8,32,256]{2,1,0:T(8,128)S(1)}, u32[]{:S(2)}, u32[]{:S(2)}) %collective-permute-start.5) | collective-permute-done | bytes 262176 | tf_op jit(solution)/shard_map/ppermute | solution.py:293
  26.9 3.4 %collective-permute-start.11 = (f32[4,32,256]{2,1,0:T(8,128)S(1)}, f32[4,32,256]{2,1,0:T(8,128)S(1)}, u32[]{:S(2)}, u32[]{:S(2)}) collective-permute-start(f32[4,32,256]{2,1,0:T(8,128)S(1)} %get-tuple-element.32), channel_id=1, source_target_pairs={{0,48},{1,49},{2,50},{3,51},{4,52},{5,53},{6,54},{7,55},{8,56},{9,... | collective-permute-start | bytes 393224 | tf_op jit(solution)/shard_map/ppermute | solution.py:293
  30.4 2.1 %collective-permute-start.6 = (f32[8,32,256]{2,1,0:T(8,128)S(1)}, f32[8,32,256]{2,1,0:T(8,128)S(1)}, u32[]{:S(2)}, u32[]{:S(2)}) collective-permute-start(f32[8,32,256]{2,1,0:T(8,128)S(1)} %add_add_fusion), channel_id=1, source_target_pairs={{0,64},{1,65},{2,66},{3,67},{4,68},{5,69},{6,70},{7,71},{8,72},{9,... | collective-permute-start | bytes 786440 | tf_op jit(solution)/shard_map/ppermute | solution.py:293
  32.6 1.2 %collective-permute-start.10 = (f32[8,32,256]{2,1,0:T(8,128)S(1)}, f32[8,32,256]{2,1,0:T(8,128)S(1)}, u32[]{:S(2)}, u32[]{:S(2)}) collective-permute-start(f32[8,32,256]{2,1,0:T(8,128)S(1)} %fusion.6), channel_id=1, source_target_pairs={{0,16},{1,17},{2,18},{3,19},{4,20},{5,21},{6,22},{7,23},{8,24},{9,... | collective-permute-start | bytes 786440 | tf_op jit(solution)/shard_map/ppermute | solution.py:293
  33.8 1.7 %collective-permute-start.12 = (f32[8,32,256]{2,1,0:T(8,128)S(1)}, f32[8,32,256]{2,1,0:T(8,128)S(1)}, u32[]{:S(2)}, u32[]{:S(2)}) collective-permute-start(f32[8,32,256]{2,1,0:T(8,128)S(1)} %fusion.5), channel_id=1, source_target_pairs={{0,48},{1,49},{2,50},{3,51},{4,52},{5,53},{6,54},{7,55},{8,56},{9,... | collective-permute-start | bytes 786440 | tf_op jit(solution)/shard_map/ppermute | solution.py:293
  35.5 1.7 %collective-permute-done.6 = f32[8,32,256]{2,1,0:T(8,128)S(1)} collective-permute-done((f32[8,32,256]{2,1,0:T(8,128)S(1)}, f32[8,32,256]{2,1,0:T(8,128)S(1)}, u32[]{:S(2)}, u32[]{:S(2)}) %collective-permute-start.6) | collective-permute-done | bytes 262176 | tf_op jit(solution)/shard_map/ppermute | solution.py:293
  37.3 2.1 %collective-permute-done.10 = f32[8,32,256]{2,1,0:T(8,128)S(1)} collective-permute-done((f32[8,32,256]{2,1,0:T(8,128)S(1)}, f32[8,32,256]{2,1,0:T(8,128)S(1)}, u32[]{:S(2)}, u32[]{:S(2)}) %collective-permute-start.10) | collective-permute-done | bytes 262176 | tf_op jit(solution)/shard_map/ppermute | solution.py:293
  39.4 0.2 collective-permute-done.12
  39.6 0.1 fusion.4.lower_ref
  39.7 1.8 %shard_map.98 = f32[128,8,128]{2,1,0:T(8,128)} custom-call(f32[8,32,256]{2,1,0:T(8,128)S(1)} %add_add_fusion.1.upper_ref, f32[8,32,256]{2,1,0:T(8,128)S(1)} %fusion.4.lower_ref, bf16[256,256]{1,0:T(8,128)(2,1)S(1)} %copy-done.4, bf16[256,256]{1,0:T(8,128)(2,1)S(1)} %copy-done.5), custom_call_target="tpu_custom_call" | custom-call | tf_op jit(solution)/shard_map/pallas_call | solution.py:245
  41.5 13.0 %all-to-all-start = ((f32[128,8,128]{2,1,0:T(8,128)}), f32[128,8,128]{2,1,0:T(8,128)S(1)}, u32[]{:S(2)}, u32[]{:S(2)}) async-start(f32[128,8,128]{2,1,0:T(8,128)} %shard_map.98), calls=%async_computation | async-start | bytes 1048576 | tf_op jit(solution)/shard_map/all_to_all | solution.py:265
  54.4 0.1 add_convert_fusion.freq_ref
  54.5 14.0 %all-to-all-done.message_ref = f32[128,8,128]{2,1,0:T(8,128)S(1)} async-done(((f32[128,8,128]{2,1,0:T(8,128)}), f32[128,8,128]{2,1,0:T(8,128)S(1)}, u32[]{:S(2)}, u32[]{:S(2)}) %all-to-all-start) | async-done | bytes 524320 | tf_op jit(solution)/shard_map/all_to_all | solution.py:265
  68.5 5.4 %shard_map.99 = f32[128,8,128]{2,1,0:T(8,128)} custom-call(f32[2]{0:T(128)S(1)} %add_convert_fusion.freq_ref, f32[128,8,128]{2,1,0:T(8,128)S(1)} %all-to-all-done.message_ref, bf16[512,256]{1,0:T(8,128)(2,1)S(1)} %copy-done, bf16[512,256]{1,0:T(8,128)(2,1)S(1)} %copy-done.1), custom_call_target="tpu_custom_call" | custom-call | tf_op jit(solution)/shard_map/pallas_call | solution.py:245
  73.9 3.9 %all-to-all-start.1 = ((f32[128,8,128]{2,1,0:T(8,128)}), f32[128,8,128]{2,1,0:T(8,128)S(1)}, u32[]{:S(2)}, u32[]{:S(2)}) async-start(f32[128,8,128]{2,1,0:T(8,128)} %shard_map.99), calls=%async_computation.1 | async-start | bytes 1048576 | tf_op jit(solution)/shard_map/all_to_all | solution.py:272
  77.8 0.8 pad_maximum_fusion
  78.7 13.3 %all-to-all-done.1.message_ref = f32[128,8,128]{2,1,0:T(8,128)S(1)} async-done(((f32[128,8,128]{2,1,0:T(8,128)}), f32[128,8,128]{2,1,0:T(8,128)S(1)}, u32[]{:S(2)}, u32[]{:S(2)}) %all-to-all-start.1) | async-done | bytes 524320 | tf_op jit(solution)/shard_map/all_to_all | solution.py:272
  91.9 1.4 %shard_map.100 = f32[16,32,256]{2,1,0:T(8,128)} custom-call(f32[128,8,128]{2,1,0:T(8,128)S(1)} %all-to-all-done.1.message_ref, bf16[256,256]{1,0:T(8,128)(2,1)S(1)} %copy-done.2, bf16[256,256]{1,0:T(8,128)(2,1)S(1)} %copy-done.3), custom_call_target="tpu_custom_call" | custom-call | tf_op jit(solution)/shard_map/pallas_call | solution.py:245
  (28 shorter events, 0.4 us)
Async XLA Ops:
  2.4 16.1 %collective-permute-start.8 = (f32[2,8,32,256]{3,2,1,0:T(8,128)S(1)}, f32[2,8,32,256]{3,2,1,0:T(8,128)S(1)}, u32[]{:S(2)}, u32[]{:S(2)}) collective-permute-start(f32[2,8,32,256]{3,2,1,0:T(8,128)S(1)} %get-tuple-element.27), channel_id=1, source_target_pairs={{0,64},{1,65},{2,66},{3,67},{4,68},{5,69},{6,70},{7,71},{8,72},{9,... | collective-permute-start | bytes 1572872 | tf_op jit(solution)/shard_map/ppermute | solution.py:293
  6.9 7.2 %collective-permute-start.4 = (f32[8,32,256]{2,1,0:T(8,128)S(1)}, f32[8,32,256]{2,1,0:T(8,128)S(1)}, u32[]{:S(2)}, u32[]{:S(2)}) collective-permute-start(f32[8,32,256]{2,1,0:T(8,128)S(1)} %get-tuple-element.23), channel_id=1, source_target_pairs={{0,48},{1,49},{2,50},{3,51},{4,52},{5,53},{6,54},{7,55},{8,56},{9,... | collective-permute-start | bytes 786440 | tf_op jit(solution)/shard_map/ppermute | solution.py:293
  9.3 8.2 %collective-permute-start = (f32[8,32,256]{2,1,0:T(8,128)S(1)}, f32[8,32,256]{2,1,0:T(8,128)S(1)}, u32[]{:S(2)}, u32[]{:S(2)}) collective-permute-start(f32[8,32,256]{2,1,0:T(8,128)S(1)} %get-tuple-element.18), channel_id=1, source_target_pairs={{0,16},{1,17},{2,18},{3,19},{4,20},{5,21},{6,22},{7,23},{8,24},{9,... | collective-permute-start | bytes 786440 | tf_op jit(solution)/shard_map/ppermute | solution.py:293
  11.0 19.4 %collective-permute-start.7 = (f32[2,8,32,256]{3,2,1,0:T(8,128)S(1)}, f32[2,8,32,256]{3,2,1,0:T(8,128)S(1)}, u32[]{:S(2)}, u32[]{:S(2)}) collective-permute-start(f32[2,8,32,256]{3,2,1,0:T(8,128)S(1)} %get-tuple-element.25), channel_id=1, source_target_pairs={{0,64},{1,65},{2,66},{3,67},{4,68},{5,69},{6,70},{7,71},{8,72},{9,... | collective-permute-start | bytes 1572872 | tf_op jit(solution)/shard_map/ppermute | solution.py:293
  11.2 28.5 %copy-start.4 = (bf16[256,256]{1,0:T(8,128)(2,1)S(1)}, bf16[256,256]{1,0:T(8,128)(2,1)}, u32[]{:S(2)}) copy-start(bf16[256,256]{1,0:T(8,128)(2,1)} %constant.29.clone.high_ref) | copy-start | bytes 393220
  11.2 28.5 %copy-start.5 = (bf16[256,256]{1,0:T(8,128)(2,1)S(1)}, bf16[256,256]{1,0:T(8,128)(2,1)}, u32[]{:S(2)}) copy-start(bf16[256,256]{1,0:T(8,128)(2,1)} %constant.30.clone.low_ref) | copy-start | bytes 393220
  11.2 57.3 %copy-start = (bf16[512,256]{1,0:T(8,128)(2,1)S(1)}, bf16[512,256]{1,0:T(8,128)(2,1)}, u32[]{:S(2)}) copy-start(bf16[512,256]{1,0:T(8,128)(2,1)} %constant.31.clone.high_ref) | copy-start | bytes 786436
  11.2 57.3 %copy-start.1 = (bf16[512,256]{1,0:T(8,128)(2,1)S(1)}, bf16[512,256]{1,0:T(8,128)(2,1)}, u32[]{:S(2)}) copy-start(bf16[512,256]{1,0:T(8,128)(2,1)} %constant.32.clone.low_ref) | copy-start | bytes 786436
  11.2 11.6 %collective-permute-start.3 = (f32[8,32,256]{2,1,0:T(8,128)S(1)}, f32[8,32,256]{2,1,0:T(8,128)S(1)}, u32[]{:S(2)}, u32[]{:S(2)}) collective-permute-start(f32[8,32,256]{2,1,0:T(8,128)S(1)} %get-tuple-element.21), channel_id=1, source_target_pairs={{0,16},{1,17},{2,18},{3,19},{4,20},{5,21},{6,22},{7,23},{8,24},{9,... | collective-permute-start | bytes 786440 | tf_op jit(solution)/shard_map/ppermute | solution.py:293
  13.9 78.0 %copy-start.2 = (bf16[256,256]{1,0:T(8,128)(2,1)S(1)}, bf16[256,256]{1,0:T(8,128)(2,1)}, u32[]{:S(2)}) copy-start(bf16[256,256]{1,0:T(8,128)(2,1)} %constant.33.clone.high_ref) | copy-start | bytes 393220
  13.9 78.0 %copy-start.3 = (bf16[256,256]{1,0:T(8,128)(2,1)S(1)}, bf16[256,256]{1,0:T(8,128)(2,1)}, u32[]{:S(2)}) copy-start(bf16[256,256]{1,0:T(8,128)(2,1)} %constant.34.clone.low_ref) | copy-start | bytes 393220
  14.1 21.4 %collective-permute-start.2 = (f32[8,32,256]{2,1,0:T(8,128)S(1)}, f32[8,32,256]{2,1,0:T(8,128)S(1)}, u32[]{:S(2)}, u32[]{:S(2)}) collective-permute-start(f32[8,32,256]{2,1,0:T(8,128)S(1)} %get-tuple-element.19), channel_id=1, source_target_pairs={{0,48},{1,49},{2,50},{3,51},{4,52},{5,53},{6,54},{7,55},{8,56},{9,... | collective-permute-start | bytes 786440 | tf_op jit(solution)/shard_map/ppermute | solution.py:293
  17.5 9.4 %collective-permute-start.5 = (f32[8,32,256]{2,1,0:T(8,128)S(1)}, f32[8,32,256]{2,1,0:T(8,128)S(1)}, u32[]{:S(2)}, u32[]{:S(2)}) collective-permute-start(f32[8,32,256]{2,1,0:T(8,128)S(1)} %add.52), channel_id=1, source_target_pairs={{0,48},{1,49},{2,50},{3,51},{4,52},{5,53},{6,54},{7,55},{8,56},{9,... | collective-permute-start | bytes 786440 | tf_op jit(solution)/shard_map/ppermute | solution.py:293
  18.5 17.0 %collective-permute-start.1 = (f32[8,32,256]{2,1,0:T(8,128)S(1)}, f32[8,32,256]{2,1,0:T(8,128)S(1)}, u32[]{:S(2)}, u32[]{:S(2)}) collective-permute-start(f32[8,32,256]{2,1,0:T(8,128)S(1)} %add.48), channel_id=1, source_target_pairs={{0,16},{1,17},{2,18},{3,19},{4,20},{5,21},{6,22},{7,23},{8,24},{9,... | collective-permute-start | bytes 786440 | tf_op jit(solution)/shard_map/ppermute | solution.py:293
  22.8 9.8 %collective-permute-start.9 = (f32[4,32,256]{2,1,0:T(8,128)S(1)}, f32[4,32,256]{2,1,0:T(8,128)S(1)}, u32[]{:S(2)}, u32[]{:S(2)}) collective-permute-start(f32[4,32,256]{2,1,0:T(8,128)S(1)} %get-tuple-element.33), channel_id=1, source_target_pairs={{0,16},{1,17},{2,18},{3,19},{4,20},{5,21},{6,22},{7,23},{8,24},{9,... | collective-permute-start | bytes 393224 | tf_op jit(solution)/shard_map/ppermute | solution.py:293
  26.9 6.8 %collective-permute-start.11 = (f32[4,32,256]{2,1,0:T(8,128)S(1)}, f32[4,32,256]{2,1,0:T(8,128)S(1)}, u32[]{:S(2)}, u32[]{:S(2)}) collective-permute-start(f32[4,32,256]{2,1,0:T(8,128)S(1)} %get-tuple-element.32), channel_id=1, source_target_pairs={{0,48},{1,49},{2,50},{3,51},{4,52},{5,53},{6,54},{7,55},{8,56},{9,... | collective-permute-start | bytes 393224 | tf_op jit(solution)/shard_map/ppermute | solution.py:293
  30.4 6.8 %collective-permute-start.6 = (f32[8,32,256]{2,1,0:T(8,128)S(1)}, f32[8,32,256]{2,1,0:T(8,128)S(1)}, u32[]{:S(2)}, u32[]{:S(2)}) collective-permute-start(f32[8,32,256]{2,1,0:T(8,128)S(1)} %add_add_fusion), channel_id=1, source_target_pairs={{0,64},{1,65},{2,66},{3,67},{4,68},{5,69},{6,70},{7,71},{8,72},{9,... | collective-permute-start | bytes 786440 | tf_op jit(solution)/shard_map/ppermute | solution.py:293
  32.6 6.8 %collective-permute-start.10 = (f32[8,32,256]{2,1,0:T(8,128)S(1)}, f32[8,32,256]{2,1,0:T(8,128)S(1)}, u32[]{:S(2)}, u32[]{:S(2)}) collective-permute-start(f32[8,32,256]{2,1,0:T(8,128)S(1)} %fusion.6), channel_id=1, source_target_pairs={{0,16},{1,17},{2,18},{3,19},{4,20},{5,21},{6,22},{7,23},{8,24},{9,... | collective-permute-start | bytes 786440 | tf_op jit(solution)/shard_map/ppermute | solution.py:293
  33.8 5.8 %collective-permute-start.12 = (f32[8,32,256]{2,1,0:T(8,128)S(1)}, f32[8,32,256]{2,1,0:T(8,128)S(1)}, u32[]{:S(2)}, u32[]{:S(2)}) collective-permute-start(f32[8,32,256]{2,1,0:T(8,128)S(1)} %fusion.5), channel_id=1, source_target_pairs={{0,48},{1,49},{2,50},{3,51},{4,52},{5,53},{6,54},{7,55},{8,56},{9,... | collective-permute-start | bytes 786440 | tf_op jit(solution)/shard_map/ppermute | solution.py:293
  41.5 27.0 %all-to-all-start = ((f32[128,8,128]{2,1,0:T(8,128)}), f32[128,8,128]{2,1,0:T(8,128)S(1)}, u32[]{:S(2)}, u32[]{:S(2)}) async-start(f32[128,8,128]{2,1,0:T(8,128)} %shard_map.98), calls=%async_computation | async-start | bytes 1048576 | tf_op jit(solution)/shard_map/all_to_all | solution.py:265
  73.9 18.0 %all-to-all-start.1 = ((f32[128,8,128]{2,1,0:T(8,128)}), f32[128,8,128]{2,1,0:T(8,128)S(1)}, u32[]{:S(2)}, u32[]{:S(2)}) async-start(f32[128,8,128]{2,1,0:T(8,128)} %shard_map.99), calls=%async_computation.1 | async-start | bytes 1048576 | tf_op jit(solution)/shard_map/all_to_all | solution.py:272

commit v2 on v1

--- a/solution.py
+++ b/solution.py
@@ -11,7 +11,8 @@
 
 spacing = 0.08
 axes = ("band", "slab")
-piece_bytes = 512 << 10
+planes = (9, 7)
+piece_bytes = 576 << 10
 spare_bytes = 4 << 20
 
 
@@ -87,7 +88,9 @@
 
 
 def forward_kernel(upper_ref, lower_ref, high_ref, low_ref, out_ref):
-    rows = jnp.concatenate([half[zq] for zq in range(8) for half in (upper_ref, lower_ref)], axis=0)
+    cut = planes[0]
+    planes_of = [upper_ref[z] if z < cut else lower_ref[z - cut] for z in range(16)]
+    rows = jnp.concatenate([planes_of[zh * 8 + zq] for zq in range(8) for zh in range(2)], axis=0)
     mean = jnp.sum(rows) * (1.0 / rows.size)
     lines = dot3((high_ref[...], low_ref[...]), split(rows - mean), rows_rows)
     zero = lax.broadcasted_iota(jnp.int32, (128, 512), 0) == 0
@@ -195,8 +198,10 @@
     rank = lax.axis_index("band")
     for slot, (half, dx, dz) in enumerate(flat):
         block = (rank + 4 * dz) // 4 % 2 * 4 + (rank + dx) % 4
-        source = orbitals_ref.at[:, pl.ds(half * 8, 8), pl.ds(block * 32, 32), :]
-        copies.append(pltpu.make_async_copy(source, buffer.at[slot], sems.at[slot]))
+        depth = planes[half]
+        source = orbitals_ref.at[:, pl.ds(half * planes[0], depth), pl.ds(block * 32, 32), :]
+        target = buffer.at[slot, :, pl.ds(0, depth)]
+        copies.append(pltpu.make_async_copy(source, target, sems.at[slot]))
     weigh = pltpu.make_async_copy(occupation_ref, weights_ref, sems.at[len(flat)])
     for copy in [weigh, *copies]:
         copy.start()
@@ -208,7 +213,7 @@
             copies[slot].wait()
             total = None
             for band in range(4):
-                values = buffer[slot, band].astype(jnp.float32)
+                values = buffer[slot, band, : planes[group[place][0]]].astype(jnp.float32)
                 term = values * values * weights[band]
                 total = term if total is None else total + term
             if len(group) == 1:
@@ -220,7 +225,7 @@
 
 def partial_densities(orbitals, occupation, pieces):
     shapes = [
-        pltpu.VMEM((8, 32, 256) if len(g) == 1 else (len(g), 8, 32, 256), jnp.float32)
+        pltpu.VMEM((len(g),) * (len(g) > 1) + (planes[g[0][0]], 32, 256), jnp.float32)
         for g in pieces
     ]
     count = sum(len(g) for g in pieces)
@@ -231,7 +236,7 @@
         in_specs=[pl.BlockSpec(memory_space=pltpu.HBM)] * 2,
         out_specs=[pl.BlockSpec(memory_space=pltpu.VMEM)] * len(shapes),
         scratch_shapes=[
-            pltpu.VMEM((count, 4, 8, 32, 256), jnp.bfloat16),
+            pltpu.VMEM((count, 4, max(planes), 32, 256), jnp.bfloat16),
             pltpu.SMEM((4,), jnp.float32),
             pltpu.SemaphoreType.DMA((count + 1,)),
         ],
@@ -296,10 +301,11 @@
     far0 = send(far0, 1, 0)
     far1 = send(far1, -1, 0)
     cross0 = send(cross0, 0, 1)
-    right1, left0, cross1 = partial_densities(orbitals, occupation, [[(0, 1, 1)], [(0, 3, 0)], [(1, 3, 1), (1, 0, 1)]])
+    right1, left0, cross3, cross4 = partial_densities(
+        orbitals, occupation, [[(0, 1, 1)], [(0, 3, 0)], [(1, 3, 1)], [(1, 0, 1)]]
+    )
     from_left1 = send(right1, 1, 0)
     from_right0 = send(left0, -1, 0)
-    cross1 = send(cross1, 0, 1)
     right0, left1, own0, own1, line2, line1, line3, line0 = partial_densities(
         orbitals,
         occupation,
@@ -307,16 +313,21 @@
     )
     from_left0 = send(right0 + far0, 1, 0)
     from_right1 = send(left1 + far1, -1, 0)
+    cross3 = send(cross3, 0, 1)
+    cross4 = send(cross4, 0, 1)
+    half = planes[1] // 2 + 1
     line2 = line2 + cross0[0]
-    ahead = send(line2[:4], 1, 0)
-    behind = send(line2[4:], -1, 0)
+    ahead = send(line2[:half], 1, 0)
+    behind = send(line2[half:], -1, 0)
     line1 = line1 + cross0[1]
-    lines1 = send(lax.dynamic_update_slice(line1, line1[:4] + ahead, (0, 0, 0)), 1, 0)
-    line3 = line3 + cross1[0]
-    lines3 = send(lax.dynamic_update_slice(line3, line3[4:] + behind, (4, 0, 0)), -1, 0)
+    line1 = lax.dynamic_update_slice(line1, line1[:half] + ahead, (0, 0, 0))
+    lines1 = send(line1, 1, 0)
+    line3 = line3 + cross3
+    line3 = lax.dynamic_update_slice(line3, line3[half:] + behind, (half, 0, 0))
+    lines3 = send(line3, -1, 0)
     other = send(own1 + from_left1 + from_right1, 0, 1)
     upper = ((own0 + from_left0) + from_right0) + other
-    lower = (line0 + cross1[1]) + (lines1 + lines3)
+    lower = (line0 + cross4) + (lines1 + lines3)
     return upper, lower
 
 

time: 93.6 us -> 101 us (1.079)
  starting transfers between devices: 37.8 us -> 41.9 us
  waiting for transfers between devices: 39 us -> 41.7 us
    ppermute x13 -> x14, waiting for transfers between devices: 11.7 us -> 14.5 us  [send(): return lax.ppermute(values, axes, ring(dx, dz))]
    ppermute x13 -> x14, starting transfers between devices: 20.9 us -> 22.9 us  [send(): return lax.ppermute(values, axes, ring(dx, dz))]
    all_to_all x2, starting transfers between devices: 16.9 us -> 18.9 us  [solve(): message = lax.all_to_all(message, axes, 0, 0, tiled=True)]
  transfers between devices with their start and end apart: 15 -> 16, of which waited for: 9 -> 6; matrix products, arithmetic and copies ran while one was open for 1% -> 1% of each run, Pallas kernels for 4% -> 4%
where the time goes in v2:
time: 101 us; the launch traced here: 100 us
  starting transfers between devices  41.9 us (41%)
  waiting for transfers between devices  41.7 us (41%)
  Pallas kernels  14.4 us (14%)
  other arithmetic  1.35 us (1%)
    all_to_all x2, waiting for transfers between devices, solve(): message = lax.all_to_all(message, axes, 0, 0, tiled=True)  27.3 us
    ppermute x14, starting transfers between devices, send(): return lax.ppermute(values, axes, ring(dx, dz))  22.9 us
    all_to_all x2, starting transfers between devices, solve(): message = lax.all_to_all(message, axes, 0, 0, tiled=True)  18.9 us
    ppermute x14, waiting for transfers between devices, send(): return lax.ppermute(values, axes, ring(dx, dz))  14.5 us
    pallas_call x3, Pallas kernels, vmem_call(): pl.pallas_call(kernel, out_shape=out_shape, in_specs=[pl.BlockSpec(memory...  8.54 us
    pallas_call x3, Pallas kernels, partial_densities(): pl.pallas_call(lambda *refs: density_kernel(pieces, *refs), out_shape=sha...  5.89 us
  transfers between devices with their start and end apart: 16, of which 6 were waited for; matrix products, arithmetic and copies ran while one was open for 1% of the time, Pallas kernels for 4%

profile of v2, /device:TPU:1, one launch (start us, length us, event | category | flops | bytes accessed | tf_op | source)
XLA Modules:
  0.0 100.3 jit_solution(2451923487921592316)
XLA Ops:
  0.6 1.7 %shard_map.96 = (f32[9,32,256]{2,1,0:T(8,128)S(1)}, f32[9,32,256]{2,1,0:T(8,128)S(1)}, f32[2,7,32,256]{3,2,1,0:T(8,128)S(1)}) custom-call(f32[4]{0:T(128)} %refs_0_.5, bf16[4,16,256,256]{3,2,1,0:T(8,128)(2,1)} %refs_1_.5), custom_call_target="tpu_custom_call" | custom-call | tf_op jit(solution)/shard_map/pallas_call | solution.py:233
  2.3 4.5 %collective-permute-start.8 = (f32[2,7,32,256]{3,2,1,0:T(8,128)S(1)}, f32[2,7,32,256]{3,2,1,0:T(8,128)S(1)}, u32[]{:S(2)}, u32[]{:S(2)}) collective-permute-start(f32[2,7,32,256]{3,2,1,0:T(8,128)S(1)} %get-tuple-element.28), channel_id=1, source_target_pairs={{0,64},{1,65},{2,66},{3,67},{4,68},{5,69},{6,70},{7,71},{8,72},{9,... | collective-permute-start | bytes 1376264 | tf_op jit(solution)/shard_map/ppermute | solution.py:298
  6.8 1.7 %shard_map.97 = (f32[9,32,256]{2,1,0:T(8,128)S(1)}, f32[9,32,256]{2,1,0:T(8,128)S(1)}, f32[7,32,256]{2,1,0:T(8,128)S(1)}, f32[7,32,256]{2,1,0:T(8,128)S(1)}) custom-call(f32[4]{0:T(128)} %refs_0_.5, bf16[4,16,256,256]{3,2,1,0:T(8,128)(2,1)} %refs_1_.5), custom_call_target="tpu_custom_call" | custom-call | tf_op jit(solution)/shard_map/pallas_call | solution.py:233
  8.5 0.1 collective-permute-start.11
  8.7 2.5 %collective-permute-start.4 = (f32[9,32,256]{2,1,0:T(8,128)S(1)}, f32[9,32,256]{2,1,0:T(8,128)S(1)}, u32[]{:S(2)}, u32[]{:S(2)}) collective-permute-start(f32[9,32,256]{2,1,0:T(8,128)S(1)} %get-tuple-element.24), channel_id=1, source_target_pairs={{0,48},{1,49},{2,50},{3,51},{4,52},{5,53},{6,54},{7,55},{8,56},{9,... | collective-permute-start | bytes 884744 | tf_op jit(solution)/shard_map/ppermute | solution.py:298
  11.2 0.1 collective-permute-start
  11.3 2.5 %shard_map.95 = (f32[9,32,256]{2,1,0:T(8,128)S(1)}, f32[9,32,256]{2,1,0:T(8,128)S(1)}, f32[9,32,256]{2,1,0:T(8,128)S(1)}, f32[9,32,256]{2,1,0:T(8,128)S(1)}, f32...) custom-call(f32[4]{0:T(128)} %refs_0_.5, ...), custom_call_target="tpu_custom_call" | custom-call | tf_op jit(solution)/shard_map/pallas_call | solution.py:233
  13.8 3.3 %collective-permute-done.8 = f32[2,7,32,256]{3,2,1,0:T(8,128)S(1)} collective-permute-done((f32[2,7,32,256]{3,2,1,0:T(8,128)S(1)}, f32[2,7,32,256]{3,2,1,0:T(8,128)S(1)}, u32[]{:S(2)}, u32[]{:S(2)}) %collective-permute-start.8) | collective-permute-done | bytes 458784 | tf_op jit(solution)/shard_map/ppermute | solution.py:298
  17.1 0.1 fusion
  17.2 2.5 %collective-permute-start.12 = (f32[3,32,256]{2,1,0:T(8,128)S(1)}, f32[3,32,256]{2,1,0:T(8,128)S(1)}, u32[]{:S(2)}, u32[]{:S(2)}) collective-permute-start(f32[3,32,256]{2,1,0:T(8,128)S(1)} %slice.29), channel_id=1, source_target_pairs={{0,48},{1,49},{2,50},{3,51},{4,52},{5,53},{6,54},{7,55},{8,56},{9,... | collective-permute-start | bytes 294920 | tf_op jit(solution)/shard_map/ppermute | solution.py:298
  19.7 2.7 %collective-permute-start.7 = (f32[7,32,256]{2,1,0:T(8,128)S(1)}, f32[7,32,256]{2,1,0:T(8,128)S(1)}, u32[]{:S(2)}, u32[]{:S(2)}) collective-permute-start(f32[7,32,256]{2,1,0:T(8,128)S(1)} %get-tuple-element.26), channel_id=1, source_target_pairs={{0,64},{1,65},{2,66},{3,67},{4,68},{5,69},{6,70},{7,71},{8,72},{9,... | collective-permute-start | bytes 688136 | tf_op jit(solution)/shard_map/ppermute | solution.py:298
  22.4 0.8 collective-permute-start.3
  23.2 1.9 %collective-permute-start.2 = (f32[9,32,256]{2,1,0:T(8,128)S(1)}, f32[9,32,256]{2,1,0:T(8,128)S(1)}, u32[]{:S(2)}, u32[]{:S(2)}) collective-permute-start(f32[9,32,256]{2,1,0:T(8,128)S(1)} %get-tuple-element.20), channel_id=1, source_target_pairs={{0,48},{1,49},{2,50},{3,51},{4,52},{5,53},{6,54},{7,55},{8,56},{9,... | collective-permute-start | bytes 884744 | tf_op jit(solution)/shard_map/ppermute | solution.py:298
  25.2 0.9 collective-permute-start.5
  26.2 0.7 collective-permute-start.9
  26.9 6.1 %collective-permute-done.9 = f32[4,32,256]{2,1,0:T(8,128)S(1)} collective-permute-done((f32[4,32,256]{2,1,0:T(8,128)S(1)}, f32[4,32,256]{2,1,0:T(8,128)S(1)}, u32[]{:S(2)}, u32[]{:S(2)}) %collective-permute-start.9) | collective-permute-done | bytes 131104 | tf_op jit(solution)/shard_map/ppermute | solution.py:298
  33.1 2.7 %collective-permute-start.13 = (f32[7,32,256]{2,1,0:T(8,128)S(1)}, f32[7,32,256]{2,1,0:T(8,128)S(1)}, u32[]{:S(2)}, u32[]{:S(2)}) collective-permute-start(f32[7,32,256]{2,1,0:T(8,128)S(1)} %fusion.3), channel_id=1, source_target_pairs={{0,48},{1,49},{2,50},{3,51},{4,52},{5,53},{6,54},{7,55},{8,56},{9,... | collective-permute-start | bytes 688136 | tf_op jit(solution)/shard_map/ppermute | solution.py:298
  35.8 1.2 %collective-permute-start.10 = (f32[7,32,256]{2,1,0:T(8,128)S(1)}, f32[7,32,256]{2,1,0:T(8,128)S(1)}, u32[]{:S(2)}, u32[]{:S(2)}) collective-permute-start(f32[7,32,256]{2,1,0:T(8,128)S(1)} %fusion.2), channel_id=1, source_target_pairs={{0,16},{1,17},{2,18},{3,19},{4,20},{5,21},{6,22},{7,23},{8,24},{9,... | collective-permute-start | bytes 688136 | tf_op jit(solution)/shard_map/ppermute | solution.py:298
  37.1 2.2 %collective-permute-start.6 = (f32[9,32,256]{2,1,0:T(8,128)S(1)}, f32[9,32,256]{2,1,0:T(8,128)S(1)}, u32[]{:S(2)}, u32[]{:S(2)}) collective-permute-start(f32[9,32,256]{2,1,0:T(8,128)S(1)} %add_add_fusion), channel_id=1, source_target_pairs={{0,64},{1,65},{2,66},{3,67},{4,68},{5,69},{6,70},{7,71},{8,72},{9,... | collective-permute-start | bytes 884744 | tf_op jit(solution)/shard_map/ppermute | solution.py:298
  39.3 1.9 %collective-permute-done.13 = f32[7,32,256]{2,1,0:T(8,128)S(1)} collective-permute-done((f32[7,32,256]{2,1,0:T(8,128)S(1)}, f32[7,32,256]{2,1,0:T(8,128)S(1)}, u32[]{:S(2)}, u32[]{:S(2)}) %collective-permute-start.13) | collective-permute-done | bytes 229408 | tf_op jit(solution)/shard_map/ppermute | solution.py:298
  41.2 3.2 %collective-permute-done.10 = f32[7,32,256]{2,1,0:T(8,128)S(1)} collective-permute-done((f32[7,32,256]{2,1,0:T(8,128)S(1)}, f32[7,32,256]{2,1,0:T(8,128)S(1)}, u32[]{:S(2)}, u32[]{:S(2)}) %collective-permute-start.10) | collective-permute-done | bytes 229408 | tf_op jit(solution)/shard_map/ppermute | solution.py:298
  44.4 0.1 add_add_fusion.2.lower_ref
  44.5 0.1 add_add_fusion.1.upper_ref
  44.6 1.8 %shard_map.98 = f32[128,8,128]{2,1,0:T(8,128)} custom-call(f32[9,32,256]{2,1,0:T(8,128)S(1)} %add_add_fusion.1.upper_ref, f32[7,32,256]{2,1,0:T(8,128)S(1)} %add_add_fusion.2.lower_ref, bf16[256,256]{1,0:T(8,128)(2,1)S(1)} %copy-done.4, bf16[256,256]{1,0:T(8,128)(2,1)S(1)} %copy-done.5), custom_call_target="tpu_custom_call" | custom-call | tf_op jit(solution)/shard_map/pallas_call | solution.py:250
  46.4 15.0 %all-to-all-start = ((f32[128,8,128]{2,1,0:T(8,128)}), f32[128,8,128]{2,1,0:T(8,128)S(1)}, u32[]{:S(2)}, u32[]{:S(2)}) async-start(f32[128,8,128]{2,1,0:T(8,128)} %shard_map.98), calls=%async_computation | async-start | bytes 1048576 | tf_op jit(solution)/shard_map/all_to_all | solution.py:270
  61.4 0.1 add_convert_fusion.freq_ref
  61.5 14.0 %all-to-all-done.message_ref = f32[128,8,128]{2,1,0:T(8,128)S(1)} async-done(((f32[128,8,128]{2,1,0:T(8,128)}), f32[128,8,128]{2,1,0:T(8,128)S(1)}, u32[]{:S(2)}, u32[]{:S(2)}) %all-to-all-start) | async-done | bytes 524320 | tf_op jit(solution)/shard_map/all_to_all | solution.py:270
  75.4 5.4 %shard_map.99 = f32[128,8,128]{2,1,0:T(8,128)} custom-call(f32[2]{0:T(128)S(1)} %add_convert_fusion.freq_ref, f32[128,8,128]{2,1,0:T(8,128)S(1)} %all-to-all-done.message_ref, bf16[512,256]{1,0:T(8,128)(2,1)S(1)} %copy-done, bf16[512,256]{1,0:T(8,128)(2,1)S(1)} %copy-done.1), custom_call_target="tpu_custom_call" | custom-call | tf_op jit(solution)/shard_map/pallas_call | solution.py:250
  80.9 3.9 %all-to-all-start.1 = ((f32[128,8,128]{2,1,0:T(8,128)}), f32[128,8,128]{2,1,0:T(8,128)S(1)}, u32[]{:S(2)}, u32[]{:S(2)}) async-start(f32[128,8,128]{2,1,0:T(8,128)} %shard_map.99), calls=%async_computation.1 | async-start | bytes 1048576 | tf_op jit(solution)/shard_map/all_to_all | solution.py:277
  84.8 0.8 pad_maximum_fusion
  85.6 13.3 %all-to-all-done.1.message_ref = f32[128,8,128]{2,1,0:T(8,128)S(1)} async-done(((f32[128,8,128]{2,1,0:T(8,128)}), f32[128,8,128]{2,1,0:T(8,128)S(1)}, u32[]{:S(2)}, u32[]{:S(2)}) %all-to-all-start.1) | async-done | bytes 524320 | tf_op jit(solution)/shard_map/all_to_all | solution.py:277
  98.9 1.4 %shard_map.100 = f32[16,32,256]{2,1,0:T(8,128)} custom-call(f32[128,8,128]{2,1,0:T(8,128)S(1)} %all-to-all-done.1.message_ref, bf16[256,256]{1,0:T(8,128)(2,1)S(1)} %copy-done.2, bf16[256,256]{1,0:T(8,128)(2,1)S(1)} %copy-done.3), custom_call_target="tpu_custom_call" | custom-call | tf_op jit(solution)/shard_map/pallas_call | solution.py:250
  (31 shorter events, 0.3 us)
Async XLA Ops:
  2.3 14.7 %collective-permute-start.8 = (f32[2,7,32,256]{3,2,1,0:T(8,128)S(1)}, f32[2,7,32,256]{3,2,1,0:T(8,128)S(1)}, u32[]{:S(2)}, u32[]{:S(2)}) collective-permute-start(f32[2,7,32,256]{3,2,1,0:T(8,128)S(1)} %get-tuple-element.28), channel_id=1, source_target_pairs={{0,64},{1,65},{2,66},{3,67},{4,68},{5,69},{6,70},{7,71},{8,72},{9,... | collective-permute-start | bytes 1376264 | tf_op jit(solution)/shard_map/ppermute | solution.py:298
  8.5 13.9 %collective-permute-start.11 = (f32[7,32,256]{2,1,0:T(8,128)S(1)}, f32[7,32,256]{2,1,0:T(8,128)S(1)}, u32[]{:S(2)}, u32[]{:S(2)}) collective-permute-start(f32[7,32,256]{2,1,0:T(8,128)S(1)} %get-tuple-element.31), channel_id=1, source_target_pairs={{0,64},{1,65},{2,66},{3,67},{4,68},{5,69},{6,70},{7,71},{8,72},{9,... | collective-permute-start | bytes 688136 | tf_op jit(solution)/shard_map/ppermute | solution.py:298
  8.7 14.6 %collective-permute-start.4 = (f32[9,32,256]{2,1,0:T(8,128)S(1)}, f32[9,32,256]{2,1,0:T(8,128)S(1)}, u32[]{:S(2)}, u32[]{:S(2)}) collective-permute-start(f32[9,32,256]{2,1,0:T(8,128)S(1)} %get-tuple-element.24), channel_id=1, source_target_pairs={{0,48},{1,49},{2,50},{3,51},{4,52},{5,53},{6,54},{7,55},{8,56},{9,... | collective-permute-start | bytes 884744 | tf_op jit(solution)/shard_map/ppermute | solution.py:298
  11.2 33.4 %copy-start.4 = (bf16[256,256]{1,0:T(8,128)(2,1)S(1)}, bf16[256,256]{1,0:T(8,128)(2,1)}, u32[]{:S(2)}) copy-start(bf16[256,256]{1,0:T(8,128)(2,1)} %constant.29.clone.high_ref) | copy-start | bytes 393220
  11.2 33.4 %copy-start.5 = (bf16[256,256]{1,0:T(8,128)(2,1)S(1)}, bf16[256,256]{1,0:T(8,128)(2,1)}, u32[]{:S(2)}) copy-start(bf16[256,256]{1,0:T(8,128)(2,1)} %constant.30.clone.low_ref) | copy-start | bytes 393220
  11.2 64.3 %copy-start = (bf16[512,256]{1,0:T(8,128)(2,1)S(1)}, bf16[512,256]{1,0:T(8,128)(2,1)}, u32[]{:S(2)}) copy-start(bf16[512,256]{1,0:T(8,128)(2,1)} %constant.31.clone.high_ref) | copy-start | bytes 786436
  11.2 64.3 %copy-start.1 = (bf16[512,256]{1,0:T(8,128)(2,1)S(1)}, bf16[512,256]{1,0:T(8,128)(2,1)}, u32[]{:S(2)}) copy-start(bf16[512,256]{1,0:T(8,128)(2,1)} %constant.32.clone.low_ref) | copy-start | bytes 786436
  11.2 14.0 %collective-permute-start = (f32[9,32,256]{2,1,0:T(8,128)S(1)}, f32[9,32,256]{2,1,0:T(8,128)S(1)}, u32[]{:S(2)}, u32[]{:S(2)}) collective-permute-start(f32[9,32,256]{2,1,0:T(8,128)S(1)} %get-tuple-element.19), channel_id=1, source_target_pairs={{0,16},{1,17},{2,18},{3,19},{4,20},{5,21},{6,22},{7,23},{8,24},{9,... | collective-permute-start | bytes 884744 | tf_op jit(solution)/shard_map/ppermute | solution.py:298
  13.8 85.1 %copy-start.2 = (bf16[256,256]{1,0:T(8,128)(2,1)S(1)}, bf16[256,256]{1,0:T(8,128)(2,1)}, u32[]{:S(2)}) copy-start(bf16[256,256]{1,0:T(8,128)(2,1)} %constant.33.clone.high_ref) | copy-start | bytes 393220
  13.8 85.1 %copy-start.3 = (bf16[256,256]{1,0:T(8,128)(2,1)S(1)}, bf16[256,256]{1,0:T(8,128)(2,1)}, u32[]{:S(2)}) copy-start(bf16[256,256]{1,0:T(8,128)(2,1)} %constant.34.clone.low_ref) | copy-start | bytes 393220
  17.2 9.1 %collective-permute-start.12 = (f32[3,32,256]{2,1,0:T(8,128)S(1)}, f32[3,32,256]{2,1,0:T(8,128)S(1)}, u32[]{:S(2)}, u32[]{:S(2)}) collective-permute-start(f32[3,32,256]{2,1,0:T(8,128)S(1)} %slice.29), channel_id=1, source_target_pairs={{0,48},{1,49},{2,50},{3,51},{4,52},{5,53},{6,54},{7,55},{8,56},{9,... | collective-permute-start | bytes 294920 | tf_op jit(solution)/shard_map/ppermute | solution.py:298
  19.7 17.4 %collective-permute-start.7 = (f32[7,32,256]{2,1,0:T(8,128)S(1)}, f32[7,32,256]{2,1,0:T(8,128)S(1)}, u32[]{:S(2)}, u32[]{:S(2)}) collective-permute-start(f32[7,32,256]{2,1,0:T(8,128)S(1)} %get-tuple-element.26), channel_id=1, source_target_pairs={{0,64},{1,65},{2,66},{3,67},{4,68},{5,69},{6,70},{7,71},{8,72},{9,... | collective-permute-start | bytes 688136 | tf_op jit(solution)/shard_map/ppermute | solution.py:298
  22.4 10.7 %collective-permute-start.3 = (f32[9,32,256]{2,1,0:T(8,128)S(1)}, f32[9,32,256]{2,1,0:T(8,128)S(1)}, u32[]{:S(2)}, u32[]{:S(2)}) collective-permute-start(f32[9,32,256]{2,1,0:T(8,128)S(1)} %get-tuple-element.22), channel_id=1, source_target_pairs={{0,16},{1,17},{2,18},{3,19},{4,20},{5,21},{6,22},{7,23},{8,24},{9,... | collective-permute-start | bytes 884744 | tf_op jit(solution)/shard_map/ppermute | solution.py:298
  23.2 21.2 %collective-permute-start.2 = (f32[9,32,256]{2,1,0:T(8,128)S(1)}, f32[9,32,256]{2,1,0:T(8,128)S(1)}, u32[]{:S(2)}, u32[]{:S(2)}) collective-permute-start(f32[9,32,256]{2,1,0:T(8,128)S(1)} %get-tuple-element.20), channel_id=1, source_target_pairs={{0,48},{1,49},{2,50},{3,51},{4,52},{5,53},{6,54},{7,55},{8,56},{9,... | collective-permute-start | bytes 884744 | tf_op jit(solution)/shard_map/ppermute | solution.py:298
  25.2 10.6 %collective-permute-start.5 = (f32[9,32,256]{2,1,0:T(8,128)S(1)}, f32[9,32,256]{2,1,0:T(8,128)S(1)}, u32[]{:S(2)}, u32[]{:S(2)}) collective-permute-start(f32[9,32,256]{2,1,0:T(8,128)S(1)} %add.52), channel_id=1, source_target_pairs={{0,48},{1,49},{2,50},{3,51},{4,52},{5,53},{6,54},{7,55},{8,56},{9,... | collective-permute-start | bytes 884744 | tf_op jit(solution)/shard_map/ppermute | solution.py:298
  26.2 6.8 %collective-permute-start.9 = (f32[4,32,256]{2,1,0:T(8,128)S(1)}, f32[4,32,256]{2,1,0:T(8,128)S(1)}, u32[]{:S(2)}, u32[]{:S(2)}) collective-permute-start(f32[4,32,256]{2,1,0:T(8,128)S(1)} %slice.27), channel_id=1, source_target_pairs={{0,16},{1,17},{2,18},{3,19},{4,20},{5,21},{6,22},{7,23},{8,24},{9,... | collective-permute-start | bytes 393224 | tf_op jit(solution)/shard_map/ppermute | solution.py:298
  33.0 11.5 %collective-permute-start.1 = (f32[9,32,256]{2,1,0:T(8,128)S(1)}, f32[9,32,256]{2,1,0:T(8,128)S(1)}, u32[]{:S(2)}, u32[]{:S(2)}) collective-permute-start(f32[9,32,256]{2,1,0:T(8,128)S(1)} %add.48), channel_id=1, source_target_pairs={{0,16},{1,17},{2,18},{3,19},{4,20},{5,21},{6,22},{7,23},{8,24},{9,... | collective-permute-start | bytes 884744 | tf_op jit(solution)/shard_map/ppermute | solution.py:298
  33.1 8.1 %collective-permute-start.13 = (f32[7,32,256]{2,1,0:T(8,128)S(1)}, f32[7,32,256]{2,1,0:T(8,128)S(1)}, u32[]{:S(2)}, u32[]{:S(2)}) collective-permute-start(f32[7,32,256]{2,1,0:T(8,128)S(1)} %fusion.3), channel_id=1, source_target_pairs={{0,48},{1,49},{2,50},{3,51},{4,52},{5,53},{6,54},{7,55},{8,56},{9,... | collective-permute-start | bytes 688136 | tf_op jit(solution)/shard_map/ppermute | solution.py:298
  35.8 8.6 %collective-permute-start.10 = (f32[7,32,256]{2,1,0:T(8,128)S(1)}, f32[7,32,256]{2,1,0:T(8,128)S(1)}, u32[]{:S(2)}, u32[]{:S(2)}) collective-permute-start(f32[7,32,256]{2,1,0:T(8,128)S(1)} %fusion.2), channel_id=1, source_target_pairs={{0,16},{1,17},{2,18},{3,19},{4,20},{5,21},{6,22},{7,23},{8,24},{9,... | collective-permute-start | bytes 688136 | tf_op jit(solution)/shard_map/ppermute | solution.py:298
  37.1 7.4 %collective-permute-start.6 = (f32[9,32,256]{2,1,0:T(8,128)S(1)}, f32[9,32,256]{2,1,0:T(8,128)S(1)}, u32[]{:S(2)}, u32[]{:S(2)}) collective-permute-start(f32[9,32,256]{2,1,0:T(8,128)S(1)} %add_add_fusion), channel_id=1, source_target_pairs={{0,64},{1,65},{2,66},{3,67},{4,68},{5,69},{6,70},{7,71},{8,72},{9,... | collective-permute-start | bytes 884744 | tf_op jit(solution)/shard_map/ppermute | solution.py:298
  46.4 29.1 %all-to-all-start = ((f32[128,8,128]{2,1,0:T(8,128)}), f32[128,8,128]{2,1,0:T(8,128)S(1)}, u32[]{:S(2)}, u32[]{:S(2)}) async-start(f32[128,8,128]{2,1,0:T(8,128)} %shard_map.98), calls=%async_computation | async-start | bytes 1048576 | tf_op jit(solution)/shard_map/all_to_all | solution.py:270
  80.9 18.0 %all-to-all-start.1 = ((f32[128,8,128]{2,1,0:T(8,128)}), f32[128,8,128]{2,1,0:T(8,128)S(1)}, u32[]{:S(2)}, u32[]{:S(2)}) async-start(f32[128,8,128]{2,1,0:T(8,128)} %shard_map.99), calls=%async_computation.1 | async-start | bytes 1048576 | tf_op jit(solution)/shard_map/all_to_all | solution.py:277

commit v3 on v2

--- a/solution.py
+++ b/solution.py
@@ -78,13 +78,11 @@
                 jnp.where(even, pltpu.roll(first, 96, axis), second),
             )
         )
-    (a0, a1), (b0, b1) = pairs
-    return (
-        jnp.where(low, a0, pltpu.roll(b0, 64, axis)),
-        jnp.where(low, a1, pltpu.roll(b1, 64, axis)),
-        jnp.where(low, pltpu.roll(a0, 64, axis), b0),
-        jnp.where(low, pltpu.roll(a1, 64, axis), b1),
-    )
+    results = []
+    for first, second in zip(*pairs):
+        turned = pltpu.roll(jnp.where(low, second, first), 64, axis)
+        results.append((jnp.where(low, first, turned), jnp.where(low, turned, second)))
+    return [pair[0] for pair in results] + [pair[1] for pair in results]
 
 
 def forward_kernel(upper_ref, lower_ref, high_ref, low_ref, out_ref):
@@ -100,58 +98,54 @@
     for pair in range(4):
         a = real[:, pair * 128 : (pair + 1) * 128]
         b = imag[:, pair * 128 : (pair + 1) * 128]
-        out_ref[:, 2 * pair, :] = jnp.where(low, a, pltpu.roll(b, 64, 1))
-        out_ref[:, 2 * pair + 1, :] = jnp.where(low, pltpu.roll(a, 64, 1), b)
-
-
-def plane_kernel(freq_ref, message_ref, high_ref, low_ref, out_ref):
+        out_ref[pl.ds(2 * pair, 128, stride=8), :] = jnp.where(low, a, pltpu.roll(b, 64, 1))
+        out_ref[pl.ds(2 * pair + 1, 128, stride=8), :] = jnp.where(low, pltpu.roll(a, 64, 1), b)
+
+
+def plane_kernel(green_ref, message_ref, high_ref, low_ref, out_ref):
     count = 256
     stacked = (high_ref[...], low_ref[...])
     beside = [jnp.concatenate([table[:count], table[count:]], axis=1) for table in stacked]
-    columns = [[], []]
-    for group in range(2):
-        parts = [
-            message_ref[(group * 4 + member) * 16 : (group * 4 + member + 1) * 16]
-            for member in range(4)
-        ]
-        blocks = swap_blocks(parts)
-        for part in range(2):
-            whole = jnp.stack([blocks[part * 2], blocks[part * 2 + 1]], axis=1)
-            columns[part].append(whole.reshape(count, 128))
-    planes = [jnp.concatenate(columns[part], axis=1) for part in range(2)]
-    means = [jnp.sum(part) * (1.0 / count**2) for part in planes]
-    operand = split(jnp.concatenate([part - mean for part, mean in zip(planes, means)], axis=0))
-    both = dot3(operand, beside, plain)
-    by_cos, by_sin = both[:, :count], both[:, count:]
-    real = by_cos[:count] + by_sin[count:]
-    imag = by_cos[count:] - by_sin[:count]
-    operand = split(jnp.concatenate([real, imag], axis=1))
-    both = dot3(stacked, operand, plain)
+    tile = jnp.sum(message_ref[...].reshape(128, 8, 128), axis=0)
+    real_lane = lax.broadcasted_iota(jnp.int32, tile.shape, 1) < 64
+    means = [
+        jnp.sum(jnp.where(real_lane == keep, tile, 0.0)) * (1.0 / count**2) for keep in (True, False)
+    ]
+    reals, imags = [], []
+    chunks = 1
+    slabs = 16 // chunks
+    rows = count // chunks
+    for chunk in range(chunks):
+        columns = [[], []]
+        for group in range(2):
+            parts = [
+                message_ref[pl.ds((member * 16 + chunk * slabs) * 8, slabs * 8), :].reshape(
+                    slabs, 8, 128
+                )
+                for member in range(group * 4, group * 4 + 4)
+            ]
+            blocks = swap_blocks(parts)
+            for part in range(2):
+                whole = jnp.stack([blocks[part * 2], blocks[part * 2 + 1]], axis=1)
+                columns[part].append(whole.reshape(rows, 128))
+        halves = [jnp.concatenate(columns[part], axis=1) - means[part] for part in range(2)]
+        both = dot3(split(jnp.concatenate(halves, axis=0)), beside, plain)
+        by_cos, by_sin = both[:, :count], both[:, count:]
+        reals.append(by_cos[:rows] + by_sin[rows:])
+        imags.append(by_cos[rows:] - by_sin[:rows])
+    real = jnp.concatenate(reals, axis=0)
+    imag = jnp.concatenate(imags, axis=0)
+    both = dot3(stacked, split(jnp.concatenate([real, imag], axis=1)), plain)
     by_cos, by_sin = both[:count], both[count:]
     real = by_cos[:, :count] + by_sin[:, count:]
     imag = by_cos[:, count:] - by_sin[:, :count]
-
-    def signed(axis):
-        index = lax.broadcasted_iota(jnp.int32, (count, count), axis)
-        return jnp.where(index < count // 2, index, index - count).astype(jnp.float32)
-
-    freq_z = signed(0)
-    freq_x = signed(1)
-    plane_sq = freq_z * freq_z + freq_x * freq_x
-    zero = plane_sq == 0.0
+    zero = (lax.broadcasted_iota(jnp.int32, (count, count), 0) == 0) & (
+        lax.broadcasted_iota(jnp.int32, (count, count), 1) == 0
+    )
     real = real + jnp.where(zero, means[0] * count**2, 0.0)
     imag = imag + jnp.where(zero, means[1] * count**2, 0.0)
-    scale = (2.0 * math.pi / (count * spacing)) ** 2
-
-    def green(freq_y):
-        wave_sq = scale * (plane_sq + freq_y * freq_y)
-        anchor = wave_sq == 0.0
-        return jnp.where(
-            anchor, 0.0, (4.0 * math.pi / count**3) / (wave_sq + anchor.astype(jnp.float32))
-        )
-
-    green_a = green(freq_ref[0])
-    green_b = green(freq_ref[1])
+    green_a = green_ref[0]
+    green_b = green_ref[1]
     operand = split(
         jnp.concatenate([real * green_a, imag * green_a, real * green_b, imag * green_b], axis=1)
     )
@@ -161,26 +155,46 @@
     imag_a = by_cos[:, count : 2 * count] + by_sin[:, :count]
     real_b = by_cos[:, 2 * count : 3 * count] - by_sin[:, 3 * count :]
     imag_b = by_cos[:, 3 * count :] + by_sin[:, 2 * count : 3 * count]
-    pair = jnp.concatenate(
-        [
-            jnp.concatenate([real_a, -imag_a], axis=1),
-            jnp.concatenate([imag_b, real_b], axis=1),
-        ],
-        axis=0,
-    )
-    result = dot3(split(pair), stacked, plain)
-    for group in range(2):
-        blocks = []
-        for part in range(2):
-            whole = result[part * count : (part + 1) * count, group * 128 : (group + 1) * 128]
-            whole = whole.reshape(16, 2, 8, 128)
-            blocks += [whole[:, 0], whole[:, 1]]
-        for member, values in enumerate(swap_blocks(blocks)):
-            out_ref[(group * 4 + member) * 16 : (group * 4 + member + 1) * 16] = values
+    for chunk in range(chunks):
+        piece = slice(chunk * rows, (chunk + 1) * rows)
+        pair = jnp.concatenate(
+            [
+                jnp.concatenate([real_a[piece], -imag_a[piece]], axis=1),
+                jnp.concatenate([imag_b[piece], real_b[piece]], axis=1),
+            ],
+            axis=0,
+        )
+        result = dot3(split(pair), stacked, plain)
+        for group in range(2):
+            blocks = []
+            for part in range(2):
+                whole = result[part * rows : (part + 1) * rows, group * 128 : (group + 1) * 128]
+                whole = whole.reshape(slabs, 2, 8, 128)
+                blocks += [whole[:, 0], whole[:, 1]]
+            for member, values in enumerate(swap_blocks(blocks), group * 4):
+                place = pl.ds((member * 16 + chunk * slabs) * 8, slabs * 8)
+                out_ref[place, :] = values.reshape(slabs * 8, 128)
+
+
+def green_planes(rank, count):
+    def signed(axis):
+        index = lax.broadcasted_iota(jnp.int32, (2, count, count), axis)
+        return jnp.where(index < count // 2, index, index - count).astype(jnp.float32)
+
+    freq_z, freq_x = signed(1), signed(2)
+    second = lax.broadcasted_iota(jnp.int32, (2, count, count), 0) == 1
+    freq_y = jnp.where(second & (rank == 0), count // 2, rank).astype(jnp.float32)
+    scale = (2.0 * math.pi / (count * spacing)) ** 2
+    wave_sq = scale * (freq_z * freq_z + freq_x * freq_x + freq_y * freq_y)
+    anchor = wave_sq == 0.0
+    inverse_points = 1.0 / count**3
+    return jnp.where(
+        anchor, 0.0, 4.0 * math.pi * inverse_points / (wave_sq + anchor.astype(jnp.float32))
+    )
 
 
 def inverse_kernel(message_ref, high_ref, low_ref, out_ref):
-    turned = [message_ref[:, zq, :].T for zq in range(8)]
+    turned = [message_ref[pl.ds(zq, 128, stride=8), :].T for zq in range(8)]
     rows = jnp.concatenate(
         [jnp.concatenate([block[:64] for block in turned], axis=0),
          jnp.concatenate([block[64:] for block in turned], axis=0)], axis=1
@@ -244,16 +258,20 @@
     )(*[pltpu.with_memory_space_constraint(value, pltpu.HBM) for value in (occupation, orbitals)])
 
 
-def vmem_call(kernel, out_shape, limit, operands, scalars=0):
-    placed = [pltpu.with_memory_space_constraint(value, pltpu.VMEM) for value in operands[scalars:]]
+def vmem_call(kernel, out_shape, limit, operands):
+    placed = [pltpu.with_memory_space_constraint(value, pltpu.VMEM) for value in operands]
     vmem = pl.BlockSpec(memory_space=pltpu.VMEM)
     return pl.pallas_call(
         kernel,
         out_shape=out_shape,
-        in_specs=[pl.BlockSpec(memory_space=pltpu.SMEM)] * scalars + [vmem] * len(placed),
+        in_specs=[vmem] * len(placed),
         out_specs=jax.tree.map(lambda shape: vmem, out_shape),
         compiler_params=pltpu.CompilerParams(vmem_limit_bytes=limit),
-    )(*operands[:scalars], *placed)
+    )(*placed)
+
+
+def exchange(message):
+    return lax.all_to_all(message, axes, 0, 0, tiled=True)
 
 
 def solve(orbitals, occupation):
@@ -264,17 +282,17 @@
     forward_real, forward_imag = line_tables(count)
     tables = split_table(np.concatenate([forward_real, forward_imag]))
     block = jax.ShapeDtypeStruct((16, 32, count), jnp.float32)
-    exchanged = pltpu.VMEM((half, 8, 128), jnp.float32)
+    exchanged = pltpu.VMEM((half * 8, 128), jnp.float32)
     message = vmem_call(forward_kernel, exchanged, 12 << 20, (upper, lower, *tables))
     density = jnp.concatenate([upper, lower], axis=0)
-    message = lax.all_to_all(message, axes, 0, 0, tiled=True)
-
     rank = lax.axis_index("band") * lax.axis_size("slab") + lax.axis_index("slab")
-    freq = jnp.stack([rank, jnp.where(rank == 0, half, rank)]).astype(jnp.float32)
+    rank, message = lax.optimization_barrier((rank, message))
+    green = green_planes(rank, count)
+    message = exchange(message)
     cosine, sine = dft_tables(count)
     tables = split_table(np.concatenate([cosine, sine]))
-    message = vmem_call(plane_kernel, exchanged, 24 << 20, (freq, message, *tables), 1)
-    message = lax.all_to_all(message, axes, 0, 0, tiled=True)
+    message = vmem_call(plane_kernel, exchanged, 24 << 20, (green, message, *tables))
+    message = exchange(message)
 
     weight = np.full((half, 1), 2.0)
     weight[0] = 1.0
@@ -297,29 +315,42 @@
     def send(values, dx, dz):
         return lax.ppermute(values, axes, ring(dx, dz))
 
-    far0, far1, cross0 = partial_densities(orbitals, occupation, [[(0, 2, 0)], [(0, 2, 1)], [(1, 2, 1), (1, 1, 1)]])
+    far0, far1, cross2 = partial_densities(
+        orbitals, occupation, [[(0, 2, 0)], [(0, 2, 1)], [(1, 2, 1)]]
+    )
     far0 = send(far0, 1, 0)
     far1 = send(far1, -1, 0)
-    cross0 = send(cross0, 0, 1)
-    right1, left0, cross3, cross4 = partial_densities(
-        orbitals, occupation, [[(0, 1, 1)], [(0, 3, 0)], [(1, 3, 1)], [(1, 0, 1)]]
-    )
+    cross2 = send(cross2, 0, 1)
+    cross1, right1, left0, cross3 = partial_densities(
+        orbitals, occupation, [[(1, 1, 1)], [(0, 1, 1)], [(0, 3, 0)], [(1, 3, 1)]]
+    )
+    cross1 = send(cross1, 0, 1)
     from_left1 = send(right1, 1, 0)
     from_right0 = send(left0, -1, 0)
-    right0, left1, own0, own1, line2, line1, line3, line0 = partial_densities(
+    left1, right0, line2, cross4, line1, line3, own1, own0, line0 = partial_densities(
         orbitals,
         occupation,
-        [[(0, 1, 0)], [(0, 3, 1)], [(0, 0, 0)], [(0, 0, 1)], [(1, 2, 0)], [(1, 1, 0)], [(1, 3, 0)], [(1, 0, 0)]],
+        [
+            [(0, 3, 1)],
+            [(0, 1, 0)],
+            [(1, 2, 0)],
+            [(1, 0, 1)],
+            [(1, 1, 0)],
+            [(1, 3, 0)],
+            [(0, 0, 1)],
+            [(0, 0, 0)],
+            [(1, 0, 0)],
+        ],
     )
     from_left0 = send(right0 + far0, 1, 0)
     from_right1 = send(left1 + far1, -1, 0)
     cross3 = send(cross3, 0, 1)
     cross4 = send(cross4, 0, 1)
     half = planes[1] // 2 + 1
-    line2 = line2 + cross0[0]
+    line2 = line2 + cross2
     ahead = send(line2[:half], 1, 0)
     behind = send(line2[half:], -1, 0)
-    line1 = line1 + cross0[1]
+    line1 = line1 + cross1
     line1 = lax.dynamic_update_slice(line1, line1[:half] + ahead, (0, 0, 0))
     lines1 = send(line1, 1, 0)
     line3 = line3 + cross3

time: 101 us -> 102 us (level)
  waiting for transfers between devices: 41.7 us -> 36.9 us
  starting transfers between devices: 41.9 us -> 46.4 us
  other arithmetic: 1.35 us -> 4.23 us
  Pallas kernels: 14.4 us -> 13.2 us
    ppermute x14 -> x15, waiting for transfers between devices: 14.5 us -> 9.86 us  [send(): return lax.ppermute(values, axes, ring(dx, dz))]
    ppermute x14 -> x15, starting transfers between devices: 22.9 us -> 25.7 us  [send(): return lax.ppermute(values, axes, ring(dx, dz))]
    all_to_all x2, starting transfers between devices: 18.9 us -> 20.7 us  [exchange(): return lax.all_to_all(message, axes, 0, 0, tiled=True)]
    pallas_call x3, Pallas kernels: 8.54 us -> 7.37 us  [vmem_call(): pl.pallas_call(kernel, out_shape=out_shape, in_specs=[vmem] * len(placed)...]
    add x1, other arithmetic: 0.08 us -> 1.13 us  [band_sum(): upper = own0 + from_left0 + from_right0 + other]
  transfers between devices with their start and end apart: 16 -> 17, of which waited for: 6 -> 7; matrix products, arithmetic and copies ran while one was open for 1% -> 3% of each run, Pallas kernels for 4% -> 4%
where the time goes in v3:
time: 102 us
  starting transfers between devices  46.4 us (45%)
  waiting for transfers between devices  36.9 us (36%)
  Pallas kernels  13.2 us (13%)
  other arithmetic  4.23 us (4%)
    all_to_all x2, waiting for transfers between devices, exchange(): return lax.all_to_all(message, axes, 0, 0, tiled=True)  27.1 us
    ppermute x15, starting transfers between devices, send(): return lax.ppermute(values, axes, ring(dx, dz))  25.7 us
    all_to_all x2, starting transfers between devices, exchange(): return lax.all_to_all(message, axes, 0, 0, tiled=True)  20.7 us
    ppermute x15, waiting for transfers between devices, send(): return lax.ppermute(values, axes, ring(dx, dz))  9.86 us
    pallas_call x3, Pallas kernels, vmem_call(): pl.pallas_call(kernel, out_shape=out_shape, in_specs=[vmem] * len(placed)...  7.37 us
    pallas_call x3, Pallas kernels, partial_densities(): pl.pallas_call(lambda *refs: density_kernel(pieces, *refs), out_shape=sha...  5.79 us
  transfers between devices with their start and end apart: 17, of which 7 were waited for; matrix products, arithmetic and copies ran while one was open for 3% of the time, Pallas kernels for 4%

profile of v3, /device:TPU:1, one launch (start us, length us, event | category | flops | bytes accessed | tf_op | source)
XLA Modules:
  0.0 101.6 jit_solution(9182205131449999336)
XLA Ops:
  0.6 1.6 %shard_map.96 = (f32[9,32,256]{2,1,0:T(8,128)S(1)}, f32[9,32,256]{2,1,0:T(8,128)S(1)}, f32[7,32,256]{2,1,0:T(8,128)S(1)}) custom-call(f32[4]{0:T(128)} %refs_0_.5, bf16[4,16,256,256]{3,2,1,0:T(8,128)(2,1)} %refs_1_.5), custom_call_target="tpu_custom_call" | custom-call | tf_op jit(solution)/shard_map/pallas_call | solution.py:247
  2.2 4.5 %collective-permute-start.9 = (f32[7,32,256]{2,1,0:T(8,128)S(1)}, f32[7,32,256]{2,1,0:T(8,128)S(1)}, u32[]{:S(2)}, u32[]{:S(2)}) collective-permute-start(f32[7,32,256]{2,1,0:T(8,128)S(1)} %get-tuple-element.33), channel_id=1, source_target_pairs={{0,64},{1,65},{2,66},{3,67},{4,68},{5,69},{6,70},{7,71},{8,72},{9,... | collective-permute-start | bytes 688136 | tf_op jit(solution)/shard_map/ppermute | solution.py:316
  6.7 2.5 %collective-permute-start.4 = (f32[9,32,256]{2,1,0:T(8,128)S(1)}, f32[9,32,256]{2,1,0:T(8,128)S(1)}, u32[]{:S(2)}, u32[]{:S(2)}) collective-permute-start(f32[9,32,256]{2,1,0:T(8,128)S(1)} %get-tuple-element.27), channel_id=1, source_target_pairs={{0,48},{1,49},{2,50},{3,51},{4,52},{5,53},{6,54},{7,55},{8,56},{9,... | collective-permute-start | bytes 884744 | tf_op jit(solution)/shard_map/ppermute | solution.py:316
  9.2 1.7 %shard_map.97 = (f32[7,32,256]{2,1,0:T(8,128)S(1)}, f32[9,32,256]{2,1,0:T(8,128)S(1)}, f32[9,32,256]{2,1,0:T(8,128)S(1)}, f32[7,32,256]{2,1,0:T(8,128)S(1)}) custom-call(f32[4]{0:T(128)} %refs_0_.5, bf16[4,16,256,256]{3,2,1,0:T(8,128)(2,1)} %refs_1_.5), custom_call_target="tpu_custom_call" | custom-call | tf_op jit(solution)/shard_map/pallas_call | solution.py:247
  10.9 0.2 collective-permute-start.12
  11.1 3.0 %collective-permute-start.8 = (f32[7,32,256]{2,1,0:T(8,128)S(1)}, f32[7,32,256]{2,1,0:T(8,128)S(1)}, u32[]{:S(2)}, u32[]{:S(2)}) collective-permute-start(f32[7,32,256]{2,1,0:T(8,128)S(1)} %get-tuple-element.31), channel_id=1, source_target_pairs={{0,64},{1,65},{2,66},{3,67},{4,68},{5,69},{6,70},{7,71},{8,72},{9,... | collective-permute-start | bytes 688136 | tf_op jit(solution)/shard_map/ppermute | solution.py:316
  14.0 2.5 %shard_map.95 = (f32[9,32,256]{2,1,0:T(8,128)S(1)}, f32[9,32,256]{2,1,0:T(8,128)S(1)}, f32[7,32,256]{2,1,0:T(8,128)S(1)}, f32[7,32,256]{2,1,0:T(8,128)S(1)}, f32...) custom-call(f32[4]{0:T(128)} %refs_0_.5, ...), custom_call_target="tpu_custom_call" | custom-call | tf_op jit(solution)/shard_map/pallas_call | solution.py:247
  16.7 2.7 %collective-permute-start.13 = (f32[3,32,256]{2,1,0:T(8,128)S(1)}, f32[3,32,256]{2,1,0:T(8,128)S(1)}, u32[]{:S(2)}, u32[]{:S(2)}) collective-permute-start(f32[3,32,256]{2,1,0:T(8,128)S(1)} %slice.19), channel_id=1, source_target_pairs={{0,48},{1,49},{2,50},{3,51},{4,52},{5,53},{6,54},{7,55},{8,56},{9,... | collective-permute-start | bytes 294920 | tf_op jit(solution)/shard_map/ppermute | solution.py:316
  19.4 0.5 collective-permute-start.7
  19.9 3.4 %collective-permute-done.8 = f32[7,32,256]{2,1,0:T(8,128)S(1)} collective-permute-done((f32[7,32,256]{2,1,0:T(8,128)S(1)}, f32[7,32,256]{2,1,0:T(8,128)S(1)}, u32[]{:S(2)}, u32[]{:S(2)}) %collective-permute-start.8) | collective-permute-done | bytes 229408 | tf_op jit(solution)/shard_map/ppermute | solution.py:316
  23.4 2.7 %collective-permute-start.2 = (f32[9,32,256]{2,1,0:T(8,128)S(1)}, f32[9,32,256]{2,1,0:T(8,128)S(1)}, u32[]{:S(2)}, u32[]{:S(2)}) collective-permute-start(f32[9,32,256]{2,1,0:T(8,128)S(1)} %get-tuple-element.23), channel_id=1, source_target_pairs={{0,48},{1,49},{2,50},{3,51},{4,52},{5,53},{6,54},{7,55},{8,56},{9,... | collective-permute-start | bytes 884744 | tf_op jit(solution)/shard_map/ppermute | solution.py:316
  26.2 0.1 collective-permute-start.10
  26.3 2.7 %collective-permute-start.5 = (f32[9,32,256]{2,1,0:T(8,128)S(1)}, f32[9,32,256]{2,1,0:T(8,128)S(1)}, u32[]{:S(2)}, u32[]{:S(2)}) collective-permute-start(f32[9,32,256]{2,1,0:T(8,128)S(1)} %add.65), channel_id=1, source_target_pairs={{0,48},{1,49},{2,50},{3,51},{4,52},{5,53},{6,54},{7,55},{8,56},{9,... | collective-permute-start | bytes 884744 | tf_op jit(solution)/shard_map/ppermute | solution.py:316
  29.1 3.1 %collective-permute-done.10 = f32[4,32,256]{2,1,0:T(8,128)S(1)} collective-permute-done((f32[4,32,256]{2,1,0:T(8,128)S(1)}, f32[4,32,256]{2,1,0:T(8,128)S(1)}, u32[]{:S(2)}, u32[]{:S(2)}) %collective-permute-start.10) | collective-permute-done | bytes 131104 | tf_op jit(solution)/shard_map/ppermute | solution.py:316
  32.2 2.7 %collective-permute-start.14 = (f32[7,32,256]{2,1,0:T(8,128)S(1)}, f32[7,32,256]{2,1,0:T(8,128)S(1)}, u32[]{:S(2)}, u32[]{:S(2)}) collective-permute-start(f32[7,32,256]{2,1,0:T(8,128)S(1)} %fusion.1), channel_id=1, source_target_pairs={{0,48},{1,49},{2,50},{3,51},{4,52},{5,53},{6,54},{7,55},{8,56},{9,... | collective-permute-start | bytes 688136 | tf_op jit(solution)/shard_map/ppermute | solution.py:316
  34.9 0.9 collective-permute-start.11
  35.8 0.8 add_add_fusion
  36.5 3.3 %collective-permute-start.6 = (f32[9,32,256]{2,1,0:T(8,128)}, f32[9,32,256]{2,1,0:T(8,128)}, u32[]{:S(2)}, u32[]{:S(2)}) collective-permute-start(f32[9,32,256]{2,1,0:T(8,128)} %add_add_fusion), channel_id=1, source_target_pairs={{0,64},{1,65},{2,66},{3,67},{4,68},{5,69},{6,70},{7,71},{8,72},{9,... | collective-permute-start | bytes 884744 | tf_op jit(solution)/shard_map/ppermute | solution.py:316
  39.8 0.5 collective-permute-done.14
  40.3 1.5 %collective-permute-done.11 = f32[7,32,256]{2,1,0:T(8,128)} collective-permute-done((f32[7,32,256]{2,1,0:T(8,128)S(1)}, f32[7,32,256]{2,1,0:T(8,128)}, u32[]{:S(2)}, u32[]{:S(2)}) %collective-permute-start.11) | collective-permute-done | bytes 229408 | tf_op jit(solution)/shard_map/ppermute | solution.py:316
  41.8 1.0 add_add_fusion.2.lower_ref
  42.8 1.4 %collective-permute-done.6 = f32[9,32,256]{2,1,0:T(8,128)} collective-permute-done((f32[9,32,256]{2,1,0:T(8,128)}, f32[9,32,256]{2,1,0:T(8,128)}, u32[]{:S(2)}, u32[]{:S(2)}) %collective-permute-start.6) | collective-permute-done | bytes 294944 | tf_op jit(solution)/shard_map/ppermute | solution.py:316
  44.2 1.1 %add_add_fusion.1.upper_ref = f32[9,32,256]{2,1,0:T(8,128)S(1)} fusion(f32[9,32,256]{2,1,0:T(8,128)} %collective-permute-done.6, f32[9,32,256]{2,1,0:T(8,128)S(1)} %collective-permute-done.2, f32[9,32,256]{2,1,0:T(8,128)S(1)} %get-tuple-element.20, f32[9,32,256]{2,1,0:T(8,128)} %collective-permute-done.1), kind=kLoop, calls=%fused_computation.3 | loop fusion | flops 221184 | bytes 1474560 | tf_op jit(solution)/shard_map/add | solution.py:360
  45.4 1.6 %shard_map.98 = f32[1024,128]{1,0:T(8,128)} custom-call(f32[9,32,256]{2,1,0:T(8,128)S(1)} %add_add_fusion.1.upper_ref, f32[7,32,256]{2,1,0:T(8,128)S(1)} %add_add_fusion.2.lower_ref, bf16[256,256]{1,0:T(8,128)(2,1)S(1)} %copy-done.4, bf16[256,256]{1,0:T(8,128)(2,1)S(1)} %copy-done.5), custom_call_target="tpu_custom_call" | custom-call | tf_op jit(solution)/shard_map/pallas_call | solution.py:264
  47.0 16.8 %all-to-all-start = ((f32[128,8,128]{2,1,0:T(8,128)}), f32[128,8,128]{2,1,0:T(8,128)S(1)}, u32[]{:S(2)}, u32[]{:S(2)}) async-start(f32[128,8,128]{2,1,0:T(8,128)} %bitcast), calls=%async_computation | async-start | bytes 1048576 | tf_op jit(solution)/shard_map/all_to_all | solution.py:274
  63.8 0.2 divide_select_fusion.green_ref
  64.0 13.8 %all-to-all-done = f32[128,8,128]{2,1,0:T(8,128)S(1)} async-done(((f32[128,8,128]{2,1,0:T(8,128)}), f32[128,8,128]{2,1,0:T(8,128)S(1)}, u32[]{:S(2)}, u32[]{:S(2)}) %all-to-all-start) | async-done | bytes 524320 | tf_op jit(solution)/shard_map/all_to_all | solution.py:274
  77.8 4.5 %shard_map.99 = f32[1024,128]{1,0:T(8,128)} custom-call(f32[2,256,256]{2,1,0:T(8,128)S(1)} %divide_select_fusion.green_ref, f32[1024,128]{1,0:T(8,128)S(1)} %bitcast.5, bf16[512,256]{1,0:T(8,128)(2,1)S(1)} %copy-done, bf16[512,256]{1,0:T(8,128)(2,1)S(1)} %copy-done.1), custom_call_target="tpu_custom_call" | custom-call | tf_op jit(solution)/shard_map/pallas_call | solution.py:264
  82.4 3.9 %all-to-all-start.1 = ((f32[128,8,128]{2,1,0:T(8,128)}), f32[128,8,128]{2,1,0:T(8,128)S(1)}, u32[]{:S(2)}, u32[]{:S(2)}) async-start(f32[128,8,128]{2,1,0:T(8,128)} %bitcast.2), calls=%async_computation.1 | async-start | bytes 1048576 | tf_op jit(solution)/shard_map/all_to_all | solution.py:274
  86.3 0.8 pad_maximum_fusion
  87.1 13.3 %all-to-all-done.1 = f32[128,8,128]{2,1,0:T(8,128)S(1)} async-done(((f32[128,8,128]{2,1,0:T(8,128)}), f32[128,8,128]{2,1,0:T(8,128)S(1)}, u32[]{:S(2)}, u32[]{:S(2)}) %all-to-all-start.1) | async-done | bytes 524320 | tf_op jit(solution)/shard_map/all_to_all | solution.py:274
  100.4 1.2 %shard_map.100 = f32[16,32,256]{2,1,0:T(8,128)} custom-call(f32[1024,128]{1,0:T(8,128)S(1)} %bitcast.4, bf16[256,256]{1,0:T(8,128)(2,1)S(1)} %copy-done.2, bf16[256,256]{1,0:T(8,128)(2,1)S(1)} %copy-done.3), custom_call_target="tpu_custom_call" | custom-call | tf_op jit(solution)/shard_map/pallas_call | solution.py:264
  (37 shorter events, 0.3 us)
Async XLA Ops:
  2.2 14.4 %collective-permute-start.9 = (f32[7,32,256]{2,1,0:T(8,128)S(1)}, f32[7,32,256]{2,1,0:T(8,128)S(1)}, u32[]{:S(2)}, u32[]{:S(2)}) collective-permute-start(f32[7,32,256]{2,1,0:T(8,128)S(1)} %get-tuple-element.33), channel_id=1, source_target_pairs={{0,64},{1,65},{2,66},{3,67},{4,68},{5,69},{6,70},{7,71},{8,72},{9,... | collective-permute-start | bytes 688136 | tf_op jit(solution)/shard_map/ppermute | solution.py:316
  6.7 16.7 %collective-permute-start.4 = (f32[9,32,256]{2,1,0:T(8,128)S(1)}, f32[9,32,256]{2,1,0:T(8,128)S(1)}, u32[]{:S(2)}, u32[]{:S(2)}) collective-permute-start(f32[9,32,256]{2,1,0:T(8,128)S(1)} %get-tuple-element.27), channel_id=1, source_target_pairs={{0,48},{1,49},{2,50},{3,51},{4,52},{5,53},{6,54},{7,55},{8,56},{9,... | collective-permute-start | bytes 884744 | tf_op jit(solution)/shard_map/ppermute | solution.py:316
  9.2 17.0 %collective-permute-start = (f32[9,32,256]{2,1,0:T(8,128)S(1)}, f32[9,32,256]{2,1,0:T(8,128)S(1)}, u32[]{:S(2)}, u32[]{:S(2)}) collective-permute-start(f32[9,32,256]{2,1,0:T(8,128)S(1)} %get-tuple-element.22), channel_id=1, source_target_pairs={{0,16},{1,17},{2,18},{3,19},{4,20},{5,21},{6,22},{7,23},{8,24},{9,... | collective-permute-start | bytes 884744 | tf_op jit(solution)/shard_map/ppermute | solution.py:316
  10.9 8.5 %collective-permute-start.12 = (f32[7,32,256]{2,1,0:T(8,128)S(1)}, f32[7,32,256]{2,1,0:T(8,128)S(1)}, u32[]{:S(2)}, u32[]{:S(2)}) collective-permute-start(f32[7,32,256]{2,1,0:T(8,128)S(1)} %get-tuple-element.35), channel_id=1, source_target_pairs={{0,64},{1,65},{2,66},{3,67},{4,68},{5,69},{6,70},{7,71},{8,72},{9,... | collective-permute-start | bytes 688136 | tf_op jit(solution)/shard_map/ppermute | solution.py:316
  11.1 34.3 %copy-start.4 = (bf16[256,256]{1,0:T(8,128)(2,1)S(1)}, bf16[256,256]{1,0:T(8,128)(2,1)}, u32[]{:S(2)}) copy-start(bf16[256,256]{1,0:T(8,128)(2,1)} %constant.43.clone.high_ref) | copy-start | bytes 393220
  11.1 34.3 %copy-start.5 = (bf16[256,256]{1,0:T(8,128)(2,1)S(1)}, bf16[256,256]{1,0:T(8,128)(2,1)}, u32[]{:S(2)}) copy-start(bf16[256,256]{1,0:T(8,128)(2,1)} %constant.44.clone.low_ref) | copy-start | bytes 393220
  11.1 66.8 %copy-start = (bf16[512,256]{1,0:T(8,128)(2,1)S(1)}, bf16[512,256]{1,0:T(8,128)(2,1)}, u32[]{:S(2)}) copy-start(bf16[512,256]{1,0:T(8,128)(2,1)} %constant.45.clone.high_ref) | copy-start | bytes 786436
  11.1 66.8 %copy-start.1 = (bf16[512,256]{1,0:T(8,128)(2,1)S(1)}, bf16[512,256]{1,0:T(8,128)(2,1)}, u32[]{:S(2)}) copy-start(bf16[512,256]{1,0:T(8,128)(2,1)} %constant.46.clone.low_ref) | copy-start | bytes 786436
  11.1 12.2 %collective-permute-start.8 = (f32[7,32,256]{2,1,0:T(8,128)S(1)}, f32[7,32,256]{2,1,0:T(8,128)S(1)}, u32[]{:S(2)}, u32[]{:S(2)}) collective-permute-start(f32[7,32,256]{2,1,0:T(8,128)S(1)} %get-tuple-element.31), channel_id=1, source_target_pairs={{0,64},{1,65},{2,66},{3,67},{4,68},{5,69},{6,70},{7,71},{8,72},{9,... | collective-permute-start | bytes 688136 | tf_op jit(solution)/shard_map/ppermute | solution.py:316
  16.6 83.8 %copy-start.2 = (bf16[256,256]{1,0:T(8,128)(2,1)S(1)}, bf16[256,256]{1,0:T(8,128)(2,1)}, u32[]{:S(2)}) copy-start(bf16[256,256]{1,0:T(8,128)(2,1)} %constant.47.clone.high_ref) | copy-start | bytes 393220
  16.6 83.8 %copy-start.3 = (bf16[256,256]{1,0:T(8,128)(2,1)S(1)}, bf16[256,256]{1,0:T(8,128)(2,1)}, u32[]{:S(2)}) copy-start(bf16[256,256]{1,0:T(8,128)(2,1)} %constant.48.clone.low_ref) | copy-start | bytes 393220
  16.7 9.6 %collective-permute-start.13 = (f32[3,32,256]{2,1,0:T(8,128)S(1)}, f32[3,32,256]{2,1,0:T(8,128)S(1)}, u32[]{:S(2)}, u32[]{:S(2)}) collective-permute-start(f32[3,32,256]{2,1,0:T(8,128)S(1)} %slice.19), channel_id=1, source_target_pairs={{0,48},{1,49},{2,50},{3,51},{4,52},{5,53},{6,54},{7,55},{8,56},{9,... | collective-permute-start | bytes 294920 | tf_op jit(solution)/shard_map/ppermute | solution.py:316
  19.4 17.1 %collective-permute-start.7 = (f32[7,32,256]{2,1,0:T(8,128)S(1)}, f32[7,32,256]{2,1,0:T(8,128)S(1)}, u32[]{:S(2)}, u32[]{:S(2)}) collective-permute-start(f32[7,32,256]{2,1,0:T(8,128)S(1)} %get-tuple-element.29), channel_id=1, source_target_pairs={{0,64},{1,65},{2,66},{3,67},{4,68},{5,69},{6,70},{7,71},{8,72},{9,... | collective-permute-start | bytes 688136 | tf_op jit(solution)/shard_map/ppermute | solution.py:316
  23.3 8.8 %collective-permute-start.3 = (f32[9,32,256]{2,1,0:T(8,128)S(1)}, f32[9,32,256]{2,1,0:T(8,128)S(1)}, u32[]{:S(2)}, u32[]{:S(2)}) collective-permute-start(f32[9,32,256]{2,1,0:T(8,128)S(1)} %get-tuple-element.25), channel_id=1, source_target_pairs={{0,16},{1,17},{2,18},{3,19},{4,20},{5,21},{6,22},{7,23},{8,24},{9,... | collective-permute-start | bytes 884744 | tf_op jit(solution)/shard_map/ppermute | solution.py:316
  23.4 19.4 %collective-permute-start.2 = (f32[9,32,256]{2,1,0:T(8,128)S(1)}, f32[9,32,256]{2,1,0:T(8,128)S(1)}, u32[]{:S(2)}, u32[]{:S(2)}) collective-permute-start(f32[9,32,256]{2,1,0:T(8,128)S(1)} %get-tuple-element.23), channel_id=1, source_target_pairs={{0,48},{1,49},{2,50},{3,51},{4,52},{5,53},{6,54},{7,55},{8,56},{9,... | collective-permute-start | bytes 884744 | tf_op jit(solution)/shard_map/ppermute | solution.py:316
  26.2 6.0 %collective-permute-start.10 = (f32[4,32,256]{2,1,0:T(8,128)S(1)}, f32[4,32,256]{2,1,0:T(8,128)S(1)}, u32[]{:S(2)}, u32[]{:S(2)}) collective-permute-start(f32[4,32,256]{2,1,0:T(8,128)S(1)} %slice.17), channel_id=1, source_target_pairs={{0,16},{1,17},{2,18},{3,19},{4,20},{5,21},{6,22},{7,23},{8,24},{9,... | collective-permute-start | bytes 393224 | tf_op jit(solution)/shard_map/ppermute | solution.py:316
  26.3 8.6 %collective-permute-start.5 = (f32[9,32,256]{2,1,0:T(8,128)S(1)}, f32[9,32,256]{2,1,0:T(8,128)S(1)}, u32[]{:S(2)}, u32[]{:S(2)}) collective-permute-start(f32[9,32,256]{2,1,0:T(8,128)S(1)} %add.65), channel_id=1, source_target_pairs={{0,48},{1,49},{2,50},{3,51},{4,52},{5,53},{6,54},{7,55},{8,56},{9,... | collective-permute-start | bytes 884744 | tf_op jit(solution)/shard_map/ppermute | solution.py:316
  32.1 10.7 %collective-permute-start.1 = (f32[9,32,256]{2,1,0:T(8,128)S(1)}, f32[9,32,256]{2,1,0:T(8,128)}, u32[]{:S(2)}, u32[]{:S(2)}) collective-permute-start(f32[9,32,256]{2,1,0:T(8,128)S(1)} %add.61), channel_id=1, source_target_pairs={{0,16},{1,17},{2,18},{3,19},{4,20},{5,21},{6,22},{7,23},{8,24},{9,... | collective-permute-start | bytes 884744 | tf_op jit(solution)/shard_map/ppermute | solution.py:316
  32.2 8.2 %collective-permute-start.14 = (f32[7,32,256]{2,1,0:T(8,128)S(1)}, f32[7,32,256]{2,1,0:T(8,128)S(1)}, u32[]{:S(2)}, u32[]{:S(2)}) collective-permute-start(f32[7,32,256]{2,1,0:T(8,128)S(1)} %fusion.1), channel_id=1, source_target_pairs={{0,48},{1,49},{2,50},{3,51},{4,52},{5,53},{6,54},{7,55},{8,56},{9,... | collective-permute-start | bytes 688136 | tf_op jit(solution)/shard_map/ppermute | solution.py:316
  34.9 6.9 %collective-permute-start.11 = (f32[7,32,256]{2,1,0:T(8,128)S(1)}, f32[7,32,256]{2,1,0:T(8,128)}, u32[]{:S(2)}, u32[]{:S(2)}) collective-permute-start(f32[7,32,256]{2,1,0:T(8,128)S(1)} %fusion), channel_id=1, source_target_pairs={{0,16},{1,17},{2,18},{3,19},{4,20},{5,21},{6,22},{7,23},{8,24},{9,... | collective-permute-start | bytes 688136 | tf_op jit(solution)/shard_map/ppermute | solution.py:316
  36.5 7.7 %collective-permute-start.6 = (f32[9,32,256]{2,1,0:T(8,128)}, f32[9,32,256]{2,1,0:T(8,128)}, u32[]{:S(2)}, u32[]{:S(2)}) collective-permute-start(f32[9,32,256]{2,1,0:T(8,128)} %add_add_fusion), channel_id=1, source_target_pairs={{0,64},{1,65},{2,66},{3,67},{4,68},{5,69},{6,70},{7,71},{8,72},{9,... | collective-permute-start | bytes 884744 | tf_op jit(solution)/shard_map/ppermute | solution.py:316
  47.0 30.8 %all-to-all-start = ((f32[128,8,128]{2,1,0:T(8,128)}), f32[128,8,128]{2,1,0:T(8,128)S(1)}, u32[]{:S(2)}, u32[]{:S(2)}) async-start(f32[128,8,128]{2,1,0:T(8,128)} %bitcast), calls=%async_computation | async-start | bytes 1048576 | tf_op jit(solution)/shard_map/all_to_all | solution.py:274
  82.4 18.0 %all-to-all-start.1 = ((f32[128,8,128]{2,1,0:T(8,128)}), f32[128,8,128]{2,1,0:T(8,128)S(1)}, u32[]{:S(2)}, u32[]{:S(2)}) async-start(f32[128,8,128]{2,1,0:T(8,128)} %bitcast.2), calls=%async_computation.1 | async-start | bytes 1048576 | tf_op jit(solution)/shard_map/all_to_all | solution.py:274

commit v4 on v3

--- a/solution.py
+++ b/solution.py
@@ -176,21 +176,24 @@
                 out_ref[place, :] = values.reshape(slabs * 8, 128)
 
 
-def green_planes(rank, count):
+def green_kernel(after_ref, out_ref):
+    del after_ref
+    count = 256
+    rank = lax.axis_index("band") * lax.axis_size("slab") + lax.axis_index("slab")
+
     def signed(axis):
-        index = lax.broadcasted_iota(jnp.int32, (2, count, count), axis)
+        index = lax.broadcasted_iota(jnp.int32, (count, count), axis)
         return jnp.where(index < count // 2, index, index - count).astype(jnp.float32)
 
-    freq_z, freq_x = signed(1), signed(2)
-    second = lax.broadcasted_iota(jnp.int32, (2, count, count), 0) == 1
-    freq_y = jnp.where(second & (rank == 0), count // 2, rank).astype(jnp.float32)
+    freq_z, freq_x = signed(0), signed(1)
     scale = (2.0 * math.pi / (count * spacing)) ** 2
-    wave_sq = scale * (freq_z * freq_z + freq_x * freq_x + freq_y * freq_y)
-    anchor = wave_sq == 0.0
-    inverse_points = 1.0 / count**3
-    return jnp.where(
-        anchor, 0.0, 4.0 * math.pi * inverse_points / (wave_sq + anchor.astype(jnp.float32))
-    )
+    for place, freq in enumerate((rank, jnp.where(rank == 0, count // 2, rank))):
+        freq_y = freq.astype(jnp.float32)
+        wave_sq = scale * (freq_z * freq_z + freq_x * freq_x + freq_y * freq_y)
+        anchor = wave_sq == 0.0
+        out_ref[place] = jnp.where(
+            anchor, 0.0, (4.0 * math.pi / count**3) / (wave_sq + anchor.astype(jnp.float32))
+        )
 
 
 def inverse_kernel(message_ref, high_ref, low_ref, out_ref):
@@ -285,9 +288,14 @@
     exchanged = pltpu.VMEM((half * 8, 128), jnp.float32)
     message = vmem_call(forward_kernel, exchanged, 12 << 20, (upper, lower, *tables))
     density = jnp.concatenate([upper, lower], axis=0)
-    rank = lax.axis_index("band") * lax.axis_size("slab") + lax.axis_index("slab")
-    rank, message = lax.optimization_barrier((rank, message))
-    green = green_planes(rank, count)
+    green = pl.pallas_call(
+        green_kernel,
+        out_shape=pltpu.VMEM((2, count, count), jnp.float32),
+        in_specs=[pl.BlockSpec(memory_space=pl.ANY)],
+        out_specs=pl.BlockSpec(memory_space=pltpu.VMEM),
+        compiler_params=pltpu.CompilerParams(vmem_limit_bytes=8 << 20),
+        name="green",
+    )(message)
     message = exchange(message)
     cosine, sine = dft_tables(count)
     tables = split_table(np.concatenate([cosine, sine]))

time: 102 us -> 99.9 us (0.979)
  other arithmetic: 4.23 us -> 1.29 us
    add x1, other arithmetic: 1.13 us -> 0.09 us  [band_sum(): upper = own0 + from_left0 + from_right0 + other]
  transfers between devices with their start and end apart: 17 -> 17, of which waited for: 7 -> 7; matrix products, arithmetic and copies ran while one was open for 3% -> 1% of each run, Pallas kernels for 4% -> 4%
where the time goes in v4:
time: 99.9 us; the launch traced here: 99.6 us
  starting transfers between devices  46.5 us (47%)
  waiting for transfers between devices  37.7 us (38%)
  Pallas kernels  13.3 us (13%)
  other arithmetic  1.29 us (1%)
    all_to_all x2, waiting for transfers between devices, exchange(): return lax.all_to_all(message, axes, 0, 0, tiled=True)  27.2 us
    ppermute x15, starting transfers between devices, send(): return lax.ppermute(values, axes, ring(dx, dz))  25.8 us
    all_to_all x2, starting transfers between devices, exchange(): return lax.all_to_all(message, axes, 0, 0, tiled=True)  20.7 us
    ppermute x15, waiting for transfers between devices, send(): return lax.ppermute(values, axes, ring(dx, dz))  10.5 us
    pallas_call x3, Pallas kernels, vmem_call(): pl.pallas_call(kernel, out_shape=out_shape, in_specs=[vmem] * len(placed)...  7.36 us
    pallas_call x3, Pallas kernels, partial_densities(): pl.pallas_call(lambda *refs: density_kernel(pieces, *refs), out_shape=sha...  5.79 us
  transfers between devices with their start and end apart: 17, of which 7 were waited for; matrix products, arithmetic and copies ran while one was open for 1% of the time, Pallas kernels for 4%

profile of v4, /device:TPU:1, one launch (start us, length us, event | category | flops | bytes accessed | tf_op | source)
XLA Modules:
  0.0 99.6 jit_solution(9089891232298861061)
XLA Ops:
  0.6 1.6 %shard_map.96 = (f32[9,32,256]{2,1,0:T(8,128)S(1)}, f32[9,32,256]{2,1,0:T(8,128)S(1)}, f32[7,32,256]{2,1,0:T(8,128)S(1)}) custom-call(f32[4]{0:T(128)} %refs_0_.5, bf16[4,16,256,256]{3,2,1,0:T(8,128)(2,1)} %refs_1_.5), custom_call_target="tpu_custom_call" | custom-call | tf_op jit(solution)/shard_map/pallas_call | solution.py:250
  2.2 4.5 %collective-permute-start.9 = (f32[7,32,256]{2,1,0:T(8,128)S(1)}, f32[7,32,256]{2,1,0:T(8,128)S(1)}, u32[]{:S(2)}, u32[]{:S(2)}) collective-permute-start(f32[7,32,256]{2,1,0:T(8,128)S(1)} %get-tuple-element.31), channel_id=1, source_target_pairs={{0,64},{1,65},{2,66},{3,67},{4,68},{5,69},{6,70},{7,71},{8,72},{9,... | collective-permute-start | bytes 688136 | tf_op jit(solution)/shard_map/ppermute | solution.py:324
  6.7 2.5 %collective-permute-start.4 = (f32[9,32,256]{2,1,0:T(8,128)S(1)}, f32[9,32,256]{2,1,0:T(8,128)S(1)}, u32[]{:S(2)}, u32[]{:S(2)}) collective-permute-start(f32[9,32,256]{2,1,0:T(8,128)S(1)} %get-tuple-element.25), channel_id=1, source_target_pairs={{0,48},{1,49},{2,50},{3,51},{4,52},{5,53},{6,54},{7,55},{8,56},{9,... | collective-permute-start | bytes 884744 | tf_op jit(solution)/shard_map/ppermute | solution.py:324
  9.2 1.7 %shard_map.97 = (f32[7,32,256]{2,1,0:T(8,128)S(1)}, f32[9,32,256]{2,1,0:T(8,128)S(1)}, f32[9,32,256]{2,1,0:T(8,128)S(1)}, f32[7,32,256]{2,1,0:T(8,128)S(1)}) custom-call(f32[4]{0:T(128)} %refs_0_.5, bf16[4,16,256,256]{3,2,1,0:T(8,128)(2,1)} %refs_1_.5), custom_call_target="tpu_custom_call" | custom-call | tf_op jit(solution)/shard_map/pallas_call | solution.py:250
  10.9 0.2 collective-permute-start.12
  11.1 3.0 %collective-permute-start.8 = (f32[7,32,256]{2,1,0:T(8,128)S(1)}, f32[7,32,256]{2,1,0:T(8,128)S(1)}, u32[]{:S(2)}, u32[]{:S(2)}) collective-permute-start(f32[7,32,256]{2,1,0:T(8,128)S(1)} %get-tuple-element.29), channel_id=1, source_target_pairs={{0,64},{1,65},{2,66},{3,67},{4,68},{5,69},{6,70},{7,71},{8,72},{9,... | collective-permute-start | bytes 688136 | tf_op jit(solution)/shard_map/ppermute | solution.py:324
  14.0 2.5 %shard_map.95 = (f32[9,32,256]{2,1,0:T(8,128)S(1)}, f32[9,32,256]{2,1,0:T(8,128)S(1)}, f32[7,32,256]{2,1,0:T(8,128)S(1)}, f32[7,32,256]{2,1,0:T(8,128)S(1)}, f32...) custom-call(f32[4]{0:T(128)} %refs_0_.5, ...), custom_call_target="tpu_custom_call" | custom-call | tf_op jit(solution)/shard_map/pallas_call | solution.py:250
  16.7 2.7 %collective-permute-start.13 = (f32[3,32,256]{2,1,0:T(8,128)S(1)}, f32[3,32,256]{2,1,0:T(8,128)S(1)}, u32[]{:S(2)}, u32[]{:S(2)}) collective-permute-start(f32[3,32,256]{2,1,0:T(8,128)S(1)} %slice.19), channel_id=1, source_target_pairs={{0,48},{1,49},{2,50},{3,51},{4,52},{5,53},{6,54},{7,55},{8,56},{9,... | collective-permute-start | bytes 294920 | tf_op jit(solution)/shard_map/ppermute | solution.py:324
  19.4 0.5 collective-permute-start.7
  19.9 3.4 %collective-permute-done.8 = f32[7,32,256]{2,1,0:T(8,128)S(1)} collective-permute-done((f32[7,32,256]{2,1,0:T(8,128)S(1)}, f32[7,32,256]{2,1,0:T(8,128)S(1)}, u32[]{:S(2)}, u32[]{:S(2)}) %collective-permute-start.8) | collective-permute-done | bytes 229408 | tf_op jit(solution)/shard_map/ppermute | solution.py:324
  23.4 2.7 %collective-permute-start.2 = (f32[9,32,256]{2,1,0:T(8,128)S(1)}, f32[9,32,256]{2,1,0:T(8,128)S(1)}, u32[]{:S(2)}, u32[]{:S(2)}) collective-permute-start(f32[9,32,256]{2,1,0:T(8,128)S(1)} %get-tuple-element.21), channel_id=1, source_target_pairs={{0,48},{1,49},{2,50},{3,51},{4,52},{5,53},{6,54},{7,55},{8,56},{9,... | collective-permute-start | bytes 884744 | tf_op jit(solution)/shard_map/ppermute | solution.py:324
  26.2 0.1 collective-permute-start.10
  26.3 2.7 %collective-permute-start.5 = (f32[9,32,256]{2,1,0:T(8,128)S(1)}, f32[9,32,256]{2,1,0:T(8,128)S(1)}, u32[]{:S(2)}, u32[]{:S(2)}) collective-permute-start(f32[9,32,256]{2,1,0:T(8,128)S(1)} %add.49), channel_id=1, source_target_pairs={{0,48},{1,49},{2,50},{3,51},{4,52},{5,53},{6,54},{7,55},{8,56},{9,... | collective-permute-start | bytes 884744 | tf_op jit(solution)/shard_map/ppermute | solution.py:324
  29.1 3.1 %collective-permute-done.10 = f32[4,32,256]{2,1,0:T(8,128)S(1)} collective-permute-done((f32[4,32,256]{2,1,0:T(8,128)S(1)}, f32[4,32,256]{2,1,0:T(8,128)S(1)}, u32[]{:S(2)}, u32[]{:S(2)}) %collective-permute-start.10) | collective-permute-done | bytes 131104 | tf_op jit(solution)/shard_map/ppermute | solution.py:324
  32.2 2.7 %collective-permute-start.14 = (f32[7,32,256]{2,1,0:T(8,128)S(1)}, f32[7,32,256]{2,1,0:T(8,128)S(1)}, u32[]{:S(2)}, u32[]{:S(2)}) collective-permute-start(f32[7,32,256]{2,1,0:T(8,128)S(1)} %fusion.1), channel_id=1, source_target_pairs={{0,48},{1,49},{2,50},{3,51},{4,52},{5,53},{6,54},{7,55},{8,56},{9,... | collective-permute-start | bytes 688136 | tf_op jit(solution)/shard_map/ppermute | solution.py:324
  34.9 0.9 collective-permute-start.11
  35.8 0.1 add_add_fusion
  35.8 3.3 %collective-permute-start.6 = (f32[9,32,256]{2,1,0:T(8,128)S(1)}, f32[9,32,256]{2,1,0:T(8,128)S(1)}, u32[]{:S(2)}, u32[]{:S(2)}) collective-permute-start(f32[9,32,256]{2,1,0:T(8,128)S(1)} %add_add_fusion), channel_id=1, source_target_pairs={{0,64},{1,65},{2,66},{3,67},{4,68},{5,69},{6,70},{7,71},{8,72},{9,... | collective-permute-start | bytes 884744 | tf_op jit(solution)/shard_map/ppermute | solution.py:324
  39.2 1.2 %collective-permute-done.14 = f32[7,32,256]{2,1,0:T(8,128)S(1)} collective-permute-done((f32[7,32,256]{2,1,0:T(8,128)S(1)}, f32[7,32,256]{2,1,0:T(8,128)S(1)}, u32[]{:S(2)}, u32[]{:S(2)}) %collective-permute-start.14) | collective-permute-done | bytes 229408 | tf_op jit(solution)/shard_map/ppermute | solution.py:324
  40.3 1.4 %collective-permute-done.11 = f32[7,32,256]{2,1,0:T(8,128)S(1)} collective-permute-done((f32[7,32,256]{2,1,0:T(8,128)S(1)}, f32[7,32,256]{2,1,0:T(8,128)S(1)}, u32[]{:S(2)}, u32[]{:S(2)}) %collective-permute-start.11) | collective-permute-done | bytes 229408 | tf_op jit(solution)/shard_map/ppermute | solution.py:324
  41.7 0.1 add_add_fusion.2.lower_ref
  41.8 1.5 %collective-permute-done.6 = f32[9,32,256]{2,1,0:T(8,128)S(1)} collective-permute-done((f32[9,32,256]{2,1,0:T(8,128)S(1)}, f32[9,32,256]{2,1,0:T(8,128)S(1)}, u32[]{:S(2)}, u32[]{:S(2)}) %collective-permute-start.6) | collective-permute-done | bytes 294944 | tf_op jit(solution)/shard_map/ppermute | solution.py:324
  43.3 0.1 add_add_fusion.1.upper_ref
  43.4 1.6 %shard_map.98.after_ref = f32[1024,128]{1,0:T(8,128)} custom-call(f32[9,32,256]{2,1,0:T(8,128)S(1)} %add_add_fusion.1.upper_ref, f32[7,32,256]{2,1,0:T(8,128)S(1)} %add_add_fusion.2.lower_ref, bf16[256,256]{1,0:T(8,128)(2,1)S(1)} %copy-done.4, bf16[256,256]{1,0:T(8,128)(2,1)S(1)} %copy-done.5), custom_call_target="tpu_custom_call" | custom-call | tf_op jit(solution)/shard_map/pallas_call | solution.py:267
  45.0 16.8 %all-to-all-start = ((f32[128,8,128]{2,1,0:T(8,128)}), f32[128,8,128]{2,1,0:T(8,128)S(1)}, u32[]{:S(2)}, u32[]{:S(2)}) async-start(f32[128,8,128]{2,1,0:T(8,128)} %bitcast), calls=%async_computation | async-start | bytes 1048576 | tf_op jit(solution)/shard_map/all_to_all | solution.py:277
  61.7 0.2 green.1.green_ref
  61.9 13.9 %all-to-all-done = f32[128,8,128]{2,1,0:T(8,128)S(1)} async-done(((f32[128,8,128]{2,1,0:T(8,128)}), f32[128,8,128]{2,1,0:T(8,128)S(1)}, u32[]{:S(2)}, u32[]{:S(2)}) %all-to-all-start) | async-done | bytes 524320 | tf_op jit(solution)/shard_map/all_to_all | solution.py:277
  75.8 4.5 %shard_map.99 = f32[1024,128]{1,0:T(8,128)} custom-call(f32[2,256,256]{2,1,0:T(8,128)S(1)} %green.1.green_ref, f32[1024,128]{1,0:T(8,128)S(1)} %bitcast.5, bf16[512,256]{1,0:T(8,128)(2,1)S(1)} %copy-done, bf16[512,256]{1,0:T(8,128)(2,1)S(1)} %copy-done.1), custom_call_target="tpu_custom_call" | custom-call | tf_op jit(solution)/shard_map/pallas_call | solution.py:267
  80.4 3.9 %all-to-all-start.1 = ((f32[128,8,128]{2,1,0:T(8,128)}), f32[128,8,128]{2,1,0:T(8,128)S(1)}, u32[]{:S(2)}, u32[]{:S(2)}) async-start(f32[128,8,128]{2,1,0:T(8,128)} %bitcast.2), calls=%async_computation.1 | async-start | bytes 1048576 | tf_op jit(solution)/shard_map/all_to_all | solution.py:277
  84.3 0.8 pad_maximum_fusion
  85.1 13.3 %all-to-all-done.1 = f32[128,8,128]{2,1,0:T(8,128)S(1)} async-done(((f32[128,8,128]{2,1,0:T(8,128)}), f32[128,8,128]{2,1,0:T(8,128)S(1)}, u32[]{:S(2)}, u32[]{:S(2)}) %all-to-all-start.1) | async-done | bytes 524320 | tf_op jit(solution)/shard_map/all_to_all | solution.py:277
  98.4 1.2 %shard_map.100 = f32[16,32,256]{2,1,0:T(8,128)} custom-call(f32[1024,128]{1,0:T(8,128)S(1)} %bitcast.4, bf16[256,256]{1,0:T(8,128)(2,1)S(1)} %copy-done.2, bf16[256,256]{1,0:T(8,128)(2,1)S(1)} %copy-done.3), custom_call_target="tpu_custom_call" | custom-call | tf_op jit(solution)/shard_map/pallas_call | solution.py:267
  (34 shorter events, 0.3 us)
Async XLA Ops:
  2.2 14.4 %collective-permute-start.9 = (f32[7,32,256]{2,1,0:T(8,128)S(1)}, f32[7,32,256]{2,1,0:T(8,128)S(1)}, u32[]{:S(2)}, u32[]{:S(2)}) collective-permute-start(f32[7,32,256]{2,1,0:T(8,128)S(1)} %get-tuple-element.31), channel_id=1, source_target_pairs={{0,64},{1,65},{2,66},{3,67},{4,68},{5,69},{6,70},{7,71},{8,72},{9,... | collective-permute-start | bytes 688136 | tf_op jit(solution)/shard_map/ppermute | solution.py:324
  6.7 16.7 %collective-permute-start.4 = (f32[9,32,256]{2,1,0:T(8,128)S(1)}, f32[9,32,256]{2,1,0:T(8,128)S(1)}, u32[]{:S(2)}, u32[]{:S(2)}) collective-permute-start(f32[9,32,256]{2,1,0:T(8,128)S(1)} %get-tuple-element.25), channel_id=1, source_target_pairs={{0,48},{1,49},{2,50},{3,51},{4,52},{5,53},{6,54},{7,55},{8,56},{9,... | collective-permute-start | bytes 884744 | tf_op jit(solution)/shard_map/ppermute | solution.py:324
  9.2 17.0 %collective-permute-start = (f32[9,32,256]{2,1,0:T(8,128)S(1)}, f32[9,32,256]{2,1,0:T(8,128)S(1)}, u32[]{:S(2)}, u32[]{:S(2)}) collective-permute-start(f32[9,32,256]{2,1,0:T(8,128)S(1)} %get-tuple-element.20), channel_id=1, source_target_pairs={{0,16},{1,17},{2,18},{3,19},{4,20},{5,21},{6,22},{7,23},{8,24},{9,... | collective-permute-start | bytes 884744 | tf_op jit(solution)/shard_map/ppermute | solution.py:324
  10.9 8.5 %collective-permute-start.12 = (f32[7,32,256]{2,1,0:T(8,128)S(1)}, f32[7,32,256]{2,1,0:T(8,128)S(1)}, u32[]{:S(2)}, u32[]{:S(2)}) collective-permute-start(f32[7,32,256]{2,1,0:T(8,128)S(1)} %get-tuple-element.33), channel_id=1, source_target_pairs={{0,64},{1,65},{2,66},{3,67},{4,68},{5,69},{6,70},{7,71},{8,72},{9,... | collective-permute-start | bytes 688136 | tf_op jit(solution)/shard_map/ppermute | solution.py:324
  11.1 32.3 %copy-start.4 = (bf16[256,256]{1,0:T(8,128)(2,1)S(1)}, bf16[256,256]{1,0:T(8,128)(2,1)}, u32[]{:S(2)}) copy-start(bf16[256,256]{1,0:T(8,128)(2,1)} %constant.16.clone.high_ref) | copy-start | bytes 393220
  11.1 32.3 %copy-start.5 = (bf16[256,256]{1,0:T(8,128)(2,1)S(1)}, bf16[256,256]{1,0:T(8,128)(2,1)}, u32[]{:S(2)}) copy-start(bf16[256,256]{1,0:T(8,128)(2,1)} %constant.17.clone.low_ref) | copy-start | bytes 393220
  11.1 64.8 %copy-start = (bf16[512,256]{1,0:T(8,128)(2,1)S(1)}, bf16[512,256]{1,0:T(8,128)(2,1)}, u32[]{:S(2)}) copy-start(bf16[512,256]{1,0:T(8,128)(2,1)} %constant.18.clone.high_ref) | copy-start | bytes 786436
  11.1 64.8 %copy-start.1 = (bf16[512,256]{1,0:T(8,128)(2,1)S(1)}, bf16[512,256]{1,0:T(8,128)(2,1)}, u32[]{:S(2)}) copy-start(bf16[512,256]{1,0:T(8,128)(2,1)} %constant.19.clone.low_ref) | copy-start | bytes 786436
  11.1 12.2 %collective-permute-start.8 = (f32[7,32,256]{2,1,0:T(8,128)S(1)}, f32[7,32,256]{2,1,0:T(8,128)S(1)}, u32[]{:S(2)}, u32[]{:S(2)}) collective-permute-start(f32[7,32,256]{2,1,0:T(8,128)S(1)} %get-tuple-element.29), channel_id=1, source_target_pairs={{0,64},{1,65},{2,66},{3,67},{4,68},{5,69},{6,70},{7,71},{8,72},{9,... | collective-permute-start | bytes 688136 | tf_op jit(solution)/shard_map/ppermute | solution.py:324
  16.6 81.8 %copy-start.2 = (bf16[256,256]{1,0:T(8,128)(2,1)S(1)}, bf16[256,256]{1,0:T(8,128)(2,1)}, u32[]{:S(2)}) copy-start(bf16[256,256]{1,0:T(8,128)(2,1)} %constant.20.clone.high_ref) | copy-start | bytes 393220
  16.6 81.8 %copy-start.3 = (bf16[256,256]{1,0:T(8,128)(2,1)S(1)}, bf16[256,256]{1,0:T(8,128)(2,1)}, u32[]{:S(2)}) copy-start(bf16[256,256]{1,0:T(8,128)(2,1)} %constant.21.clone.low_ref) | copy-start | bytes 393220
  16.7 9.6 %collective-permute-start.13 = (f32[3,32,256]{2,1,0:T(8,128)S(1)}, f32[3,32,256]{2,1,0:T(8,128)S(1)}, u32[]{:S(2)}, u32[]{:S(2)}) collective-permute-start(f32[3,32,256]{2,1,0:T(8,128)S(1)} %slice.19), channel_id=1, source_target_pairs={{0,48},{1,49},{2,50},{3,51},{4,52},{5,53},{6,54},{7,55},{8,56},{9,... | collective-permute-start | bytes 294920 | tf_op jit(solution)/shard_map/ppermute | solution.py:324
  19.4 16.4 %collective-permute-start.7 = (f32[7,32,256]{2,1,0:T(8,128)S(1)}, f32[7,32,256]{2,1,0:T(8,128)S(1)}, u32[]{:S(2)}, u32[]{:S(2)}) collective-permute-start(f32[7,32,256]{2,1,0:T(8,128)S(1)} %get-tuple-element.27), channel_id=1, source_target_pairs={{0,64},{1,65},{2,66},{3,67},{4,68},{5,69},{6,70},{7,71},{8,72},{9,... | collective-permute-start | bytes 688136 | tf_op jit(solution)/shard_map/ppermute | solution.py:324
  23.3 8.8 %collective-permute-start.3 = (f32[9,32,256]{2,1,0:T(8,128)S(1)}, f32[9,32,256]{2,1,0:T(8,128)S(1)}, u32[]{:S(2)}, u32[]{:S(2)}) collective-permute-start(f32[9,32,256]{2,1,0:T(8,128)S(1)} %get-tuple-element.23), channel_id=1, source_target_pairs={{0,16},{1,17},{2,18},{3,19},{4,20},{5,21},{6,22},{7,23},{8,24},{9,... | collective-permute-start | bytes 884744 | tf_op jit(solution)/shard_map/ppermute | solution.py:324
  23.4 18.4 %collective-permute-start.2 = (f32[9,32,256]{2,1,0:T(8,128)S(1)}, f32[9,32,256]{2,1,0:T(8,128)S(1)}, u32[]{:S(2)}, u32[]{:S(2)}) collective-permute-start(f32[9,32,256]{2,1,0:T(8,128)S(1)} %get-tuple-element.21), channel_id=1, source_target_pairs={{0,48},{1,49},{2,50},{3,51},{4,52},{5,53},{6,54},{7,55},{8,56},{9,... | collective-permute-start | bytes 884744 | tf_op jit(solution)/shard_map/ppermute | solution.py:324
  26.2 6.0 %collective-permute-start.10 = (f32[4,32,256]{2,1,0:T(8,128)S(1)}, f32[4,32,256]{2,1,0:T(8,128)S(1)}, u32[]{:S(2)}, u32[]{:S(2)}) collective-permute-start(f32[4,32,256]{2,1,0:T(8,128)S(1)} %slice.17), channel_id=1, source_target_pairs={{0,16},{1,17},{2,18},{3,19},{4,20},{5,21},{6,22},{7,23},{8,24},{9,... | collective-permute-start | bytes 393224 | tf_op jit(solution)/shard_map/ppermute | solution.py:324
  26.3 8.6 %collective-permute-start.5 = (f32[9,32,256]{2,1,0:T(8,128)S(1)}, f32[9,32,256]{2,1,0:T(8,128)S(1)}, u32[]{:S(2)}, u32[]{:S(2)}) collective-permute-start(f32[9,32,256]{2,1,0:T(8,128)S(1)} %add.49), channel_id=1, source_target_pairs={{0,48},{1,49},{2,50},{3,51},{4,52},{5,53},{6,54},{7,55},{8,56},{9,... | collective-permute-start | bytes 884744 | tf_op jit(solution)/shard_map/ppermute | solution.py:324
  32.1 9.7 %collective-permute-start.1 = (f32[9,32,256]{2,1,0:T(8,128)S(1)}, f32[9,32,256]{2,1,0:T(8,128)S(1)}, u32[]{:S(2)}, u32[]{:S(2)}) collective-permute-start(f32[9,32,256]{2,1,0:T(8,128)S(1)} %add.45), channel_id=1, source_target_pairs={{0,16},{1,17},{2,18},{3,19},{4,20},{5,21},{6,22},{7,23},{8,24},{9,... | collective-permute-start | bytes 884744 | tf_op jit(solution)/shard_map/ppermute | solution.py:324
  32.2 8.2 %collective-permute-start.14 = (f32[7,32,256]{2,1,0:T(8,128)S(1)}, f32[7,32,256]{2,1,0:T(8,128)S(1)}, u32[]{:S(2)}, u32[]{:S(2)}) collective-permute-start(f32[7,32,256]{2,1,0:T(8,128)S(1)} %fusion.1), channel_id=1, source_target_pairs={{0,48},{1,49},{2,50},{3,51},{4,52},{5,53},{6,54},{7,55},{8,56},{9,... | collective-permute-start | bytes 688136 | tf_op jit(solution)/shard_map/ppermute | solution.py:324
  34.9 6.8 %collective-permute-start.11 = (f32[7,32,256]{2,1,0:T(8,128)S(1)}, f32[7,32,256]{2,1,0:T(8,128)S(1)}, u32[]{:S(2)}, u32[]{:S(2)}) collective-permute-start(f32[7,32,256]{2,1,0:T(8,128)S(1)} %fusion), channel_id=1, source_target_pairs={{0,16},{1,17},{2,18},{3,19},{4,20},{5,21},{6,22},{7,23},{8,24},{9,... | collective-permute-start | bytes 688136 | tf_op jit(solution)/shard_map/ppermute | solution.py:324
  35.8 7.4 %collective-permute-start.6 = (f32[9,32,256]{2,1,0:T(8,128)S(1)}, f32[9,32,256]{2,1,0:T(8,128)S(1)}, u32[]{:S(2)}, u32[]{:S(2)}) collective-permute-start(f32[9,32,256]{2,1,0:T(8,128)S(1)} %add_add_fusion), channel_id=1, source_target_pairs={{0,64},{1,65},{2,66},{3,67},{4,68},{5,69},{6,70},{7,71},{8,72},{9,... | collective-permute-start | bytes 884744 | tf_op jit(solution)/shard_map/ppermute | solution.py:324
  45.0 30.8 %all-to-all-start = ((f32[128,8,128]{2,1,0:T(8,128)}), f32[128,8,128]{2,1,0:T(8,128)S(1)}, u32[]{:S(2)}, u32[]{:S(2)}) async-start(f32[128,8,128]{2,1,0:T(8,128)} %bitcast), calls=%async_computation | async-start | bytes 1048576 | tf_op jit(solution)/shard_map/all_to_all | solution.py:277
  80.4 18.0 %all-to-all-start.1 = ((f32[128,8,128]{2,1,0:T(8,128)}), f32[128,8,128]{2,1,0:T(8,128)S(1)}, u32[]{:S(2)}, u32[]{:S(2)}) async-start(f32[128,8,128]{2,1,0:T(8,128)} %bitcast.2), calls=%async_computation.1 | async-start | bytes 1048576 | tf_op jit(solution)/shard_map/all_to_all | solution.py:277
